TPU v7x, 32 devices: a whole 2x2x4 slice. The times are simulated.
32 devices in a mesh: batch: 4 (over y, x), layer: 8 (over z, core).
Axes of the slice: x: 2, y: 2, z: 4, core: 2. Of those that a mesh axis runs over, the one named last changes fastest.
Arguments:
- inputs: float32 [256, 1024], P(None, 'batch'), parts along dimension 1, may hold values from -6 to 6
- guess: float32 [8, 256, 1024], P('layer', None, 'batch'), parts along dimension 2, may hold values from -6 to 6
- weights: bfloat16 [32, 256, 2304], P('layer'), may hold values from -0.125 to 0.125
Outputs:
- states: float32 [32, 256, 1024], P('layer', None, 'batch'), parts along dimension 2
There are 4 independent parts, one for each index of `batch`. A program takes and returns all parts, laid end to end along the dimension named above; an argument that names none is the same for every part. Nothing has to cross between parts.
All inputs are finite; a program needn't handle non-finite values.
Results may differ from a plain program's by a relative error of at most 0.01.
Values may be sent and summed in bfloat16 or wider, within the bound.
A program may use at most 64 MiB of HBM per device.

v0:
```python
import functools

import jax
import jax.numpy as jnp
from jax import lax
from jax.experimental import pallas as pl
from jax.experimental.pallas import tpu as pltpu
from jax.sharding import PartitionSpec as P

WIDTH = 16
COARSEN = 4
LEFT, FIRST, SECOND, FINAL, CHANGE, RHS, WEIGHT, MATE, MATE_SECOND = range(9)
SLOTS = 7
SENDS = 9
PIECES = 8


def kernel(
    devices, x_hbm, g_hbm, w_hbm, o_ref,
    xg, w, pad, cp, lf, rhs, rhs_mate, tt, cc, psi, xy, xz, out,
    sent, got, send_sem, recv_sem, load_sem, weight_sem,
):
    f32, bf16 = jnp.float32, jnp.bfloat16
    p = lax.axis_index("layer")
    phase = lax.rem(p, COARSEN)
    owner = phase == COARSEN - 1
    group = lax.div(p, COARSEN)
    lead = lax.rem(p, 2) == 1
    mate = jnp.logical_not(lead)
    cells, chans = cp.shape

    loads = [
        pltpu.make_async_copy(x_hbm, xg.at[0], load_sem.at[0]),
        pltpu.make_async_copy(g_hbm.at[0], xg.at[1], load_sem.at[1]),
    ]

    def weight_loads(j):
        rows = w.shape[1] // PIECES
        return [
            pltpu.make_async_copy(
                w_hbm.at[j, pl.ds(n * rows, rows)], w.at[j, pl.ds(n * rows, rows)],
                weight_sem.at[j, n],
            )
            for n in range(PIECES)
        ]

    for load in loads:
        load.start()
    for load in weight_loads(0) + weight_loads(1):
        load.start()

    barrier = pltpu.get_barrier_semaphore()

    def greet(by, cond):
        @pl.when(cond)
        def _():
            pl.semaphore_signal(
                barrier, inc=1, device_id={"layer": p + by},
                device_id_type=pl.DeviceIdType.MESH,
            )
        return cond.astype(jnp.int32)

    has_next = p < devices - 1
    lead_next = jnp.logical_and(lead, p + 2 < devices)
    last_owner = p + COARSEN >= devices
    greeted = (
        greet(1, has_next) + greet(-1, p > 0)
        + greet(COARSEN - 1, jnp.logical_and(phase == 0, group > 0))
        + greet(1 - COARSEN, jnp.logical_and(owner, group > 0))
        + greet(2, lead_next) + greet(-2, jnp.logical_and(lead, p >= 2))
    )

    def message(slot, by, relayed=None):
        if slot == WEIGHT:
            src, dst = w.at[0], w.at[COARSEN]
        else:
            src, dst = sent.at[slot], got.at[slot]
        send_slot = slot
        if relayed is not None:
            src = got.at[relayed]
            send_slot = MATE_SECOND if slot == SECOND else MATE
        return pltpu.make_async_remote_copy(
            src_ref=src, dst_ref=dst,
            send_sem=send_sem.at[send_slot], recv_sem=recv_sem.at[slot],
            device_id={"layer": p + by}, device_id_type=pl.DeviceIdType.MESH,
        )

    def send(slot, by, cond, relayed=None):
        @pl.when(cond)
        def _():
            message(slot, by, relayed).start()

    def receive(slot, by):
        message(slot, by).wait_recv()
        return got[slot].astype(f32)

    pad[:, 0:WIDTH, :] = jnp.zeros((3, WIDTH, chans), bf16)
    pad[:, WIDTH + cells:, :] = jnp.zeros((3, WIDTH, chans), bf16)

    def bend(v, j):
        col = lax.rem(lax.broadcasted_iota(jnp.int32, v.shape, 0), WIDTH)
        zero = jnp.zeros_like(v)
        before = jnp.where(col == 0, zero, pltpu.roll(v, 1, 0))
        after = jnp.where(col == WIDTH - 1, zero, pltpu.roll(v, cells - 1, 0))
        for d, piece in enumerate((before, v, after)):
            pad[d, WIDTH:WIDTH + cells, :] = piece.astype(bf16)
        patches = jnp.concatenate([
            pad[dx, WIDTH * dy:WIDTH * dy + cells, :] for dy in range(3) for dx in range(3)
        ], 1)
        total = lax.dot_general(
            patches, w[j], (((1,), (1,)), ((), ())), preferred_element_type=f32,
        )
        return jnp.tanh(total)

    def put(n, value):
        o_ref[n] = value.T

    for load in loads:
        load.wait()
    lf[...] = jnp.where(p == 0, xg[0], xg[1]).T

    cp[...] = lf[...]
    shares = jnp.logical_and(mate, p > 0)
    owner_shares = jnp.logical_and(owner, group > 0)
    changes = jnp.logical_and(phase == 0, group > 0)

    def first_layer(j, _):
        for load in weight_loads(j):
            load.wait()

        @pl.when(j < COARSEN - 2)
        def _():
            for load in weight_loads(j + 2):
                load.start()

        @pl.when(j == 0)
        def _():
            pl.semaphore_wait(barrier, greeted)
            send(WEIGHT, 1, shares)
            send(WEIGHT, 1 - COARSEN, owner_shares)

        v = cp[...]
        cp[...] = v + 0.25 * bend(v, j)
        return 0

    lax.fori_loop(0, COARSEN, first_layer, 0)
    sent[LEFT] = cp[...].astype(bf16)
    send(LEFT, 1, has_next)

    @pl.when(p > 0)
    def _():
        lf[...] = receive(LEFT, -1)

    cc[...] = lf[...]

    def second_layer(j, _):
        v = cc[...]
        t = bend(v, j)

        @pl.when(j == 0)
        def _():
            tt[...] = t

        cc[...] = v + 0.25 * t
        return 0

    lax.fori_loop(0, COARSEN, second_layer, 0)
    resid = cc[...] - cp[...]
    rhs[...] = cp[...] - (lf[...] + tt[...]) + resid

    def whole_step(v):
        return v + bend(v, COARSEN) + rhs_mate[...]

    def finish_owner():
        second = rhs[...] - (cc[...] - psi[...])
        coarse_rhs = cc[...] - xy[...] + second
        solved = xz[...] + coarse_rhs
        upper = cc[...]
        sent[FINAL] = solved.astype(bf16)
        send(FINAL, 2, lead_next)
        sent[SECOND] = upper.astype(bf16)
        send(SECOND, 2, lead_next)
        cc[...] = solved

    def relax_second():
        v = receive(SECOND, -2)
        send(SECOND, -1, relays_upper, SECOND)
        v = whole_step(v)
        psi[...] = v + bend(v, 0)

        @pl.when(owner)
        def _():
            xz[...] = receive(CHANGE, 1 - COARSEN)
            xy[...] = jnp.zeros_like(xy)
            finish_owner()

    late = jnp.logical_and(jnp.logical_and(owner, group > 0), last_owner)
    relays_first = jnp.logical_and(owner, group == 0)
    relays_final = jnp.logical_and(lead, group > 0)
    relays_upper = jnp.logical_and(relays_final, phase == 1)

    @pl.when(mate)
    def _():
        sent[RHS] = rhs[...].astype(bf16)
        send(RHS, 1, shares)

        @pl.when(phase == 0)
        def _():
            cc[...] = lf[...] + tt[...] + rhs[...]
            sent[FIRST] = cc[...].astype(bf16)
            send(FIRST, 1, phase == 0)

        @pl.when(p > 0)
        def _():
            @pl.when(group == 0)
            def _():
                lf[...] = receive(FIRST, 1)

            @pl.when(group > 0)
            def _():
                lf[...] = receive(FINAL, 1)

            v = lf[...]
            tt[...] = bend(v, 0)
            cc[...] = v + tt[...] + rhs[...]

    @pl.when(lead)
    def _():
        @pl.when(jnp.logical_and(owner, group == 0))
        def _():
            start = xg[0].T
            xi = start + 4.0 * bend(start, 0)
            xy[...] = xi
            xz[...] = xi

        @pl.when(p > 1)
        def _():
            message(WEIGHT, -1).wait_recv()
            rhs_mate[...] = receive(RHS, -1)

        @pl.when(phase == 1)
        def _():
            lf[...] = receive(FIRST, -1)

        @pl.when(owner)
        def _():
            v = receive(FIRST, -2)
            send(FIRST, -1, relays_first, FIRST)
            lf[...] = whole_step(v)

        v = lf[...]
        tt[...] = bend(v, 0)
        psi[...] = v + tt[...]
        cc[...] = psi[...] + rhs[...]

        @pl.when(phase == 1)
        def _():
            sent[FIRST] = cc[...].astype(bf16)
            send(FIRST, 2, phase == 1)

        @pl.when(jnp.logical_and(owner, group == 0))
        def _():
            finish_owner()

        @pl.when(group > 0)
        def _():
            v = receive(FINAL, -2)
            send(FINAL, -1, relays_final, FINAL)
            v = whole_step(v)
            lf[...] = v
            tt[...] = bend(v, 0)

            @pl.when(phase == 1)
            def _():
                cc[...] = v + tt[...] + rhs[...]
                sent[FINAL] = cc[...].astype(bf16)
                send(FINAL, 2, lead_next)

            @pl.when(jnp.logical_not(late))
            def _():
                relax_second()

            @pl.when(phase == 1)
            def _():
                sent[SECOND] = (psi[...] + rhs[...]).astype(bf16)
                send(SECOND, 2, lead_next)

    out[...] = lf[...] + 0.25 * tt[...]
    put(0, out[...])

    def last_layer(j, _):
        v = out[...]
        new = v + 0.25 * bend(v, j)
        out[...] = new
        put(j, new)
        return 0

    lax.fori_loop(1, COARSEN - 1, last_layer, 0)

    @pl.when(changes)
    def _():
        message(WEIGHT, COARSEN - 1).wait_recv()
        v = lf[...]
        xz[...] = v + 4.0 * bend(v, COARSEN)
        v = receive(SECOND, 1)
        sent[CHANGE] = (xz[...] - (v + 4.0 * bend(v, COARSEN))).astype(bf16)
        send(CHANGE, COARSEN - 1, changes)

    @pl.when(late)
    def _():
        relax_second()

    put(COARSEN - 1, cc[...])

    def drain(slot, by, cond, relayed=None):
        @pl.when(cond)
        def _():
            message(slot, by, relayed).wait_send()

    relaxed = jnp.logical_or(group > 0, owner)
    drain(LEFT, 1, has_next)
    drain(WEIGHT, 1, shares)
    drain(RHS, 1, shares)
    drain(FIRST, 1, phase == 0)
    drain(FIRST, 2, phase == 1)
    drain(FIRST, -1, relays_first, FIRST)
    drain(FINAL, 2, jnp.logical_and(relaxed, lead_next))
    drain(FINAL, -1, relays_final, FINAL)
    drain(SECOND, 2, jnp.logical_and(relaxed, lead_next))
    drain(SECOND, -1, relays_upper, SECOND)
    drain(WEIGHT, 1 - COARSEN, owner_shares)
    drain(CHANGE, COARSEN - 1, changes)


def per_device(devices, inputs, guess, weights):
    chans, cells = inputs.shape
    state = pltpu.VMEM((cells, chans), jnp.float32)
    messages = pltpu.VMEM((SLOTS, cells, chans), jnp.bfloat16)
    return pl.pallas_call(
        functools.partial(kernel, devices),
        name="cycle",
        out_shape=pltpu.VMEM((COARSEN, chans, cells), jnp.float32),
        in_specs=[pl.BlockSpec(memory_space=pltpu.HBM)] * 3,
        out_specs=pl.BlockSpec(memory_space=pltpu.VMEM),
        scratch_shapes=[
            pltpu.VMEM((2, chans, cells), jnp.float32),
            pltpu.VMEM((COARSEN + 1,) + weights.shape[1:], jnp.bfloat16),
            pltpu.VMEM((3, cells + 2 * WIDTH, chans), jnp.bfloat16),
        ] + [state] * 10 + [
            messages, messages,
            pltpu.SemaphoreType.DMA((SENDS,)),
            pltpu.SemaphoreType.DMA((SLOTS,)),
            pltpu.SemaphoreType.DMA((2,)),
            pltpu.SemaphoreType.DMA((COARSEN, PIECES)),
        ],
        compiler_params=pltpu.CompilerParams(
            collective_id=0, has_side_effects=True, vmem_limit_bytes=56 * 2**20,
        ),
    )(*[pltpu.with_memory_space_constraint(a, pltpu.HBM) for a in (inputs, guess, weights)])


def solution(mesh):
    return jax.shard_map(
        functools.partial(per_device, mesh.shape["layer"]),
        mesh=mesh,
        in_specs=(P(None, "batch"), P("layer", None, "batch"), P("layer", None, None)),
        out_specs=P("layer", None, "batch"),
        check_vma=False,
    )
```

profile of v0, /device:TPU:29, one launch (start us, length us, event | category | flops | bytes accessed | tf_op | source)
XLA Modules:
  0.0 25.7 jit_solution(5505085384430701862)
XLA Ops:
  0.0 24.7 %cycle.1 = f32[4,256,256]{2,1,0:T(8,128)S(1)} custom-call(f32[256,256]{1,0:T(8,128)} %x_hbm.1, f32[1,256,256]{2,1,0:T(8,128)} %g_hbm.1, bf16[4,256,2304]{2,1,0:T(8,128)(2,1)} %w_hbm.1), custom_call_target="tpu_custom_call" | custom-call | tf_op jit(solution)/shard_map/cycle/pallas_call | solution.py:339
  24.7 1.0 %copy.5 = f32[4,256,256]{2,1,0:T(8,128)} copy(f32[4,256,256]{2,1,0:T(8,128)S(1)} %cycle.1) | data formatting | bytes 2097152
where the time goes:
time: 25.9 us; the launch traced here: 25.7 us
  Pallas kernels  24.7 us (95%)
  local copies, waits for them, and re-layouts  0.97 us (4%)
    pallas_call x1, Pallas kernels, per_device(): pl.pallas_call(functools.partial(kernel, devices), name='cycle', out_shap...  24.7 us
    unnamed x1, local copies, waits for them, and re-layouts  0.97 us

commit v1 on v0

v1 whole, which is shorter than its diff:
```python
import functools

import jax
import jax.numpy as jnp
from jax import lax
from jax.experimental import pallas as pl
from jax.experimental.pallas import tpu as pltpu
from jax.sharding import PartitionSpec as P

WIDTH = 16
COARSEN = 4
LEFT, FIRST, SECOND, FINAL, CHANGE, RHS, UNSENT, WEIGHT = range(8)
NONE = 15
SLOTS = 7
PIECES = 8
MAX_STEPS = 16
ZERO, CP, LF, CC, RH, RHM, TT, PSI, QQ, XZ, OUT, TMP, DUMP = range(13)
STATES = 13
NOTHING, PSI_OF_LEFT, FIRST_POINT, START, PUT_0, PUT_1, PUT_2, OWNER_0, OWNER, CHANGES = range(10)
FIELDS = ("src", "dst", "w", "add", "factor", "tanh", "send", "by", "recv", "relay", "need", "op")
BY_ONE, BY_TWO = 0, 1
QUARTER, WHOLE, FOUR = 0, 1, 2


def step(src, dst, w, add=ZERO, factor=QUARTER, tanh=DUMP, send=UNSENT, by=BY_ONE,
         recv=NONE, relay=0, need=0, op=NOTHING):
    return dict(src=src, dst=dst, w=w, add=add, factor=factor, tanh=tanh, send=send, by=by,
                recv=recv, relay=relay, need=need, op=op)


def programs():
    def fine(send=UNSENT, tanh=DUMP, op=NOTHING):
        return [step(CP, CP, 0, tanh=tanh), step(CP, CP, 1), step(CP, CP, 2),
                step(CP, CP, 3, send=send, op=op)]

    def again(send=UNSENT, op=NOTHING):
        return [step(LF, CC, 0, tanh=TT, recv=LEFT, op=PSI_OF_LEFT), step(CC, CC, 1),
                step(CC, CC, 2), step(CC, RH, 3, add=QQ, send=send, op=op)]

    def whole(recv, dst, relay=0, need=0):
        return step(TMP, dst, COARSEN, add=RHM, factor=WHOLE, recv=recv, relay=relay, need=need)

    def own(src, dst, **kw):
        return step(src, dst, 0, add=RH, factor=WHOLE, **kw)

    last = [step(OUT, OUT, 1, op=PUT_1), step(OUT, OUT, 2, op=PUT_2)]
    body = fine(LEFT) + again()
    mate = fine(LEFT) + again(RHS)
    final = [whole(FINAL, LF, relay=1)]
    owner_second = [whole(SECOND, TMP), step(TMP, PSI, 0, factor=WHOLE, op=OWNER)]
    relaxed = [whole(FIRST, TMP, need=1), own(TMP, CC)] + final + [
        step(LF, DUMP, 0, factor=WHOLE, tanh=TT, op=PUT_0)]
    return {
        "start": fine(LEFT, TT, START) + last,
        "lead_first": body + [own(LF, CC, tanh=TT, recv=FIRST, send=FIRST, by=BY_TWO, op=PUT_0)] + last,
        "mate_first": mate + [own(LF, CC, tanh=TT, recv=FIRST, op=PUT_0)] + last,
        "owner_first": body + [
            step(TMP, XZ, 0, factor=FOUR), whole(FIRST, LF, relay=1, need=1),
            own(LF, CC, tanh=TT, op=OWNER_0)] + last,
        "head": fine(LEFT) + again(RHS, FIRST_POINT) + [
            own(LF, CC, tanh=TT, recv=FINAL, op=PUT_0)] + last + [
            step(LF, XZ, COARSEN, factor=FOUR, need=2),
            step(TMP, TMP, COARSEN, factor=FOUR, recv=SECOND, op=CHANGES)],
        "lead": body + [
            own(LF, TMP, recv=FIRST, send=FIRST, by=BY_TWO),
            whole(FINAL, LF, relay=1, need=1),
            own(LF, CC, tanh=TT, send=FINAL, by=BY_TWO, op=PUT_0),
            whole(SECOND, TMP, relay=1),
            own(TMP, TMP, send=SECOND, by=BY_TWO)] + last,
        "mate": mate + [own(LF, CC, tanh=TT, recv=FINAL, op=PUT_0)] + last,
        "owner": body + relaxed + owner_second + last,
        "owner_last": body + relaxed + last + owner_second,
    }


def packed(values):
    words = []
    for start in (0, 8):
        word = sum(v << (4 * k) for k, v in enumerate(values[start:start + 8]))
        words.append(word - 2**32 if word >= 2**31 else word)
    return words


def kernel(
    devices, x_hbm, g_hbm, w_hbm, o_ref,
    xg, w, pad, st, sent, got,
    send_sem, relay_sem, extra_sem, recv_sem, load_sem, weight_sem,
):
    f32, bf16 = jnp.float32, jnp.bfloat16
    p = lax.axis_index("layer")
    phase = lax.rem(p, COARSEN)
    owner = phase == COARSEN - 1
    group = lax.div(p, COARSEN)
    lead = lax.rem(p, 2) == 1
    mate = jnp.logical_not(lead)
    _, cells, chans = st.shape

    own_load = pltpu.make_async_copy(g_hbm.at[0], xg.at[0], load_sem.at[0])
    x_load = pltpu.make_async_copy(x_hbm, xg.at[0], load_sem.at[0])
    start_load = pltpu.make_async_copy(x_hbm, xg.at[1], load_sem.at[1])
    first_owner = jnp.logical_and(owner, group == 0)

    def weight_loads(j):
        rows = w.shape[1] // PIECES
        return [
            pltpu.make_async_copy(
                w_hbm.at[j, pl.ds(n * rows, rows)], w.at[j, pl.ds(n * rows, rows)],
                weight_sem.at[j, n],
            )
            for n in range(PIECES)
        ]

    @pl.when(p == 0)
    def _():
        x_load.start()

    @pl.when(p > 0)
    def _():
        own_load.start()

    for load in weight_loads(0) + weight_loads(1):
        load.start()

    @pl.when(first_owner)
    def _():
        start_load.start()

    barrier = pltpu.get_barrier_semaphore()

    def greet(by, cond):
        @pl.when(cond)
        def _():
            pl.semaphore_signal(
                barrier, inc=1, device_id={"layer": p + by},
                device_id_type=pl.DeviceIdType.MESH,
            )
        return cond.astype(jnp.int32)

    has_next = p < devices - 1
    lead_next = jnp.logical_and(lead, p + 2 < devices)
    last_owner = p + COARSEN >= devices
    greeted = (
        greet(1, has_next) + greet(-1, p > 0)
        + greet(COARSEN - 1, jnp.logical_and(phase == 0, group > 0))
        + greet(1 - COARSEN, jnp.logical_and(owner, group > 0))
        + greet(2, lead_next) + greet(-2, jnp.logical_and(lead, p >= 2))
    )
    shares = jnp.logical_and(mate, p > 0)
    owner_shares = jnp.logical_and(owner, group > 0)
    changes = jnp.logical_and(phase == 0, group > 0)

    roles = [
        ("start", p == 0),
        ("lead_first", jnp.logical_and(group == 0, phase == 1)),
        ("mate_first", jnp.logical_and(group == 0, phase == 2)),
        ("owner_first", first_owner),
        ("head", changes),
        ("lead", jnp.logical_and(group > 0, phase == 1)),
        ("mate", jnp.logical_and(group > 0, phase == 2)),
        ("owner_last", jnp.logical_and(owner, jnp.logical_and(group > 0, last_owner))),
    ]
    listed = programs()

    def chosen(value_of):
        value = jnp.int32(value_of(listed["owner"]))
        for name, cond in roles:
            value = jnp.where(cond, jnp.int32(value_of(listed[name])), value)
        return value

    count = chosen(len)
    words = {
        field: [
            chosen(lambda steps: packed([s[field] for s in steps])[half]) for half in (0, 1)
        ]
        for field in FIELDS
    }

    def entry(field, i):
        low, high = words[field]
        word = jnp.where(i < 8, low, high)
        return jnp.bitwise_and(
            lax.shift_right_logical(word, 4 * jnp.bitwise_and(i, 7)), 15
        )

    def remote(src, dst, ssem, rsem, by):
        return pltpu.make_async_remote_copy(
            src_ref=src, dst_ref=dst, send_sem=ssem, recv_sem=rsem,
            device_id={"layer": p + by}, device_id_type=pl.DeviceIdType.MESH,
        )

    def message(i, slot, by):
        return remote(sent.at[slot], got.at[slot], send_sem.at[i], recv_sem.at[slot], by)

    def relay_of(i, slot):
        return remote(got.at[slot], got.at[slot], relay_sem.at[i], recv_sem.at[slot], -1)

    back = jnp.where(p > 0, -1, 1)

    def arrived(slot):
        remote(sent.at[slot], got.at[slot], extra_sem.at[0], recv_sem.at[slot], back).wait_recv()

    def weight_to(by):
        return remote(w.at[0], w.at[COARSEN], extra_sem.at[0], recv_sem.at[WEIGHT], by)

    def special(n, slot, by):
        return remote(sent.at[slot], got.at[slot], extra_sem.at[n], recv_sem.at[slot], by)

    def distance(code):
        return jnp.where(code == BY_TWO, 2, 1)

    pad[:, 0:WIDTH, :] = jnp.zeros((3, WIDTH, chans), bf16)
    pad[:, WIDTH + cells:, :] = jnp.zeros((3, WIDTH, chans), bf16)
    st[ZERO] = jnp.zeros((cells, chans), f32)

    def put(n):
        o_ref[n] = st[OUT].T

    own_load.wait()
    loaded = xg[0].T
    st[LF] = loaded
    st[CP] = loaded

    @pl.when(first_owner)
    def _():
        start_load.wait()
        st[TMP] = xg[1].T

    def finish_owner(xy):
        cc = st[CC]
        second = st[RH] - (cc - st[PSI])
        solved = st[XZ] + ((cc - st[xy]) + second)

        @pl.when(lead_next)
        def _():
            sent[FINAL] = solved.astype(bf16)
            special(1, FINAL, 2).start()
            sent[SECOND] = cc.astype(bf16)
            special(2, SECOND, 2).start()

        st[CC] = solved

    def run(i, _):
        f = {field: entry(field, i) for field in FIELDS}
        is_fine = i < COARSEN

        @pl.when(is_fine)
        def _():
            for load in weight_loads(i):
                load.wait()

            @pl.when(i < COARSEN - 2)
            def _():
                for load in weight_loads(i + 2):
                    load.start()

        @pl.when(i == 1)
        def _():
            pl.semaphore_wait(barrier, greeted)

            @pl.when(shares)
            def _():
                weight_to(1).start()

            @pl.when(owner_shares)
            def _():
                weight_to(1 - COARSEN).start()

        @pl.when(f["need"] > 0)
        def _():
            remote(w.at[0], w.at[COARSEN], extra_sem.at[0], recv_sem.at[WEIGHT], back).wait_recv()

        @pl.when(f["need"] == 1)
        def _():
            arrived(RHS)
            st[RHM] = got[RHS].astype(f32)

        @pl.when(f["recv"] != NONE)
        def _():
            arrived(f["recv"])

            @pl.when(f["relay"] == 1)
            def _():
                relay_of(i, f["recv"]).start()

            st[f["src"]] = got[f["recv"]].astype(f32)

        v = st[f["src"]]
        col = lax.rem(lax.broadcasted_iota(jnp.int32, v.shape, 0), WIDTH)
        zero = jnp.zeros_like(v)
        before = jnp.where(col == 0, zero, pltpu.roll(v, 1, 0))
        after = jnp.where(col == WIDTH - 1, zero, pltpu.roll(v, cells - 1, 0))
        for d, piece in enumerate((before, v, after)):
            pad[d, WIDTH:WIDTH + cells, :] = piece.astype(bf16)
        patches = jnp.concatenate([
            pad[dx, WIDTH * dy:WIDTH * dy + cells, :] for dy in range(3) for dx in range(3)
        ], 1)
        total = lax.dot_general(
            patches, w[f["w"]], (((1,), (1,)), ((), ())), preferred_element_type=f32,
        )
        t = jnp.tanh(total)
        factor = jnp.where(f["factor"] == QUARTER, 0.25, jnp.where(f["factor"] == WHOLE, 1.0, 4.0))
        new = (st[f["src"]] + factor * t) + st[f["add"]]
        st[f["tanh"]] = t
        st[f["dst"]] = new
        sent[f["send"]] = new.astype(bf16)

        @pl.when(jnp.logical_and(f["send"] != UNSENT, has_next))
        def _():
            message(i, f["send"], distance(f["by"])).start()

        op = f["op"]

        @pl.when(op == PSI_OF_LEFT)
        def _():
            psi = st[LF] + st[TT]
            st[PSI] = psi
            st[QQ] = (st[CP] - psi) - st[CP]

        @pl.when(op == START)
        def _():
            psi = st[LF] + st[TT]
            rhs = st[CP] + ((st[CP] - psi) - st[CP])
            first = psi + rhs
            st[CC] = first
            sent[FIRST] = first.astype(bf16)
            special(1, FIRST, 1).start()

        @pl.when(op == FIRST_POINT)
        def _():
            sent[FIRST] = (st[PSI] + st[RH]).astype(bf16)
            special(1, FIRST, 1).start()

        @pl.when(op == OWNER_0)
        def _():
            st[PSI] = st[LF] + st[TT]
            finish_owner(XZ)

        @pl.when(jnp.logical_or(op == PUT_0, jnp.logical_or(op == START, op == OWNER_0)))
        def _():
            st[OUT] = st[LF] + 0.25 * st[TT]

        put_at = jnp.where(op == PUT_1, 1, jnp.where(op == PUT_2, 2, 0))

        @pl.when(jnp.logical_and(op >= START, op <= OWNER_0))
        def _():
            put(put_at)

        @pl.when(op == OWNER)
        def _():
            arrived(CHANGE)
            st[XZ] = got[CHANGE].astype(f32)
            finish_owner(ZERO)

        @pl.when(op == CHANGES)
        def _():
            sent[CHANGE] = (st[XZ] - st[TMP]).astype(bf16)
            special(2, CHANGE, COARSEN - 1).start()

        return 0

    lax.fori_loop(0, count, run, 0)
    o_ref[COARSEN - 1] = st[CC].T

    def drain(i, _):
        slot = entry("send", i)

        @pl.when(jnp.logical_and(slot != UNSENT, has_next))
        def _():
            message(i, slot, distance(entry("by", i))).wait_send()

        @pl.when(entry("relay", i) == 1)
        def _():
            relay_of(i, entry("recv", i)).wait_send()

        return 0

    lax.fori_loop(0, count, drain, 0)

    def drain_special(copy, cond):
        @pl.when(cond)
        def _():
            copy.wait_send()

    drain_special(weight_to(1), jnp.logical_or(shares, owner_shares))
    drain_special(special(1, FIRST, 1), phase == 0)
    drain_special(special(2, CHANGE, COARSEN - 1), changes)
    sends_solved = jnp.logical_and(owner, lead_next)
    drain_special(special(1, FINAL, 2), sends_solved)
    drain_special(special(2, SECOND, 2), sends_solved)


def per_device(devices, inputs, guess, weights):
    chans, cells = inputs.shape
    messages = pltpu.VMEM((SLOTS, cells, chans), jnp.bfloat16)
    return pl.pallas_call(
        functools.partial(kernel, devices),
        name="cycle",
        out_shape=pltpu.VMEM((COARSEN, chans, cells), jnp.float32),
        in_specs=[pl.BlockSpec(memory_space=pltpu.HBM)] * 3,
        out_specs=pl.BlockSpec(memory_space=pltpu.VMEM),
        scratch_shapes=[
            pltpu.VMEM((2, chans, cells), jnp.float32),
            pltpu.VMEM((COARSEN + 1,) + weights.shape[1:], jnp.bfloat16),
            pltpu.VMEM((3, cells + 2 * WIDTH, chans), jnp.bfloat16),
            pltpu.VMEM((STATES, cells, chans), jnp.float32),
            messages, messages,
            pltpu.SemaphoreType.DMA((MAX_STEPS,)),
            pltpu.SemaphoreType.DMA((MAX_STEPS,)),
            pltpu.SemaphoreType.DMA((3,)),
            pltpu.SemaphoreType.DMA((SLOTS + 1,)),
            pltpu.SemaphoreType.DMA((2,)),
            pltpu.SemaphoreType.DMA((COARSEN, PIECES)),
        ],
        compiler_params=pltpu.CompilerParams(
            collective_id=0, has_side_effects=True, vmem_limit_bytes=56 * 2**20,
        ),
    )(*[pltpu.with_memory_space_constraint(a, pltpu.HBM) for a in (inputs, guess, weights)])


def solution(mesh):
    return jax.shard_map(
        functools.partial(per_device, mesh.shape["layer"]),
        mesh=mesh,
        in_specs=(P(None, "batch"), P("layer", None, "batch"), P("layer", None, None)),
        out_specs=P("layer", None, "batch"),
        check_vma=False,
    )
```

time: 25.9 us -> 27 us (1.042)
  Pallas kernels: 24.7 us -> 25.9 us
    pallas_call x1, Pallas kernels: 24.7 us -> 25.9 us  [per_device(): pl.pallas_call(functools.partial(kernel, devices), name='cycle', out_shap...]
where the time goes in v1:
time: 27 us; the launch traced here: 26.9 us
  Pallas kernels  25.9 us (96%)
  local copies, waits for them, and re-layouts  0.97 us (4%)
    pallas_call x1, Pallas kernels, per_device(): pl.pallas_call(functools.partial(kernel, devices), name='cycle', out_shap...  25.9 us
    unnamed x1, local copies, waits for them, and re-layouts  0.97 us

profile of v1, /device:TPU:29, one launch (start us, length us, event | category | flops | bytes accessed | tf_op | source)
XLA Modules:
  0.0 26.9 jit_solution(2265893049102979898)
XLA Ops:
  0.0 25.9 %cycle.1 = f32[4,256,256]{2,1,0:T(8,128)S(1)} custom-call(f32[256,256]{1,0:T(8,128)} %x_hbm.1, f32[1,256,256]{2,1,0:T(8,128)} %g_hbm.1, bf16[4,256,2304]{2,1,0:T(8,128)(2,1)} %w_hbm.1), custom_call_target="tpu_custom_call" | custom-call | tf_op jit(solution)/shard_map/cycle/pallas_call | solution.py:395
  25.9 1.0 %copy.5 = f32[4,256,256]{2,1,0:T(8,128)} copy(f32[4,256,256]{2,1,0:T(8,128)S(1)} %cycle.1) | data formatting | bytes 2097152

commit v2 on v1

--- a/solution.py
+++ b/solution.py
@@ -9,23 +9,30 @@
 
 WIDTH = 16
 COARSEN = 4
-LEFT, FIRST, SECOND, FINAL, CHANGE, RHS, UNSENT, WEIGHT = range(8)
 NONE = 15
-SLOTS = 7
 PIECES = 8
 MAX_STEPS = 16
+BLOCKS = 4
 ZERO, CP, LF, CC, RH, RHM, TT, PSI, QQ, XZ, OUT, TMP, DUMP = range(13)
 STATES = 13
+CPB, LFB, OUTB, CCB, TMPB, LEFT, FIRST, SECOND, FINAL, UNSENT = range(10)
+TO_LEFT, TO_FIRST, TO_SECOND, TO_FINAL, TO_CHANGE, TO_RHS, CHANGE, RHS = range(10, 18)
+ROUNDED = 18
+WEIGHT = ROUNDED
 NOTHING, PSI_OF_LEFT, FIRST_POINT, START, PUT_0, PUT_1, PUT_2, OWNER_0, OWNER, CHANGES = range(10)
-FIELDS = ("src", "dst", "w", "add", "factor", "tanh", "send", "by", "recv", "relay", "need", "op")
+FIELDS = ("src", "dst", "w", "add", "factor", "tanh", "rsrc", "rdst", "by", "recv", "relay", "need", "op")
 BY_ONE, BY_TWO = 0, 1
 QUARTER, WHOLE, FOUR = 0, 1, 2
+ROUNDED_OF = {CP: CPB, LF: LFB, CC: CCB, OUT: OUTB, TMP: TMPB}
 
 
 def step(src, dst, w, add=ZERO, factor=QUARTER, tanh=DUMP, send=UNSENT, by=BY_ONE,
-         recv=NONE, relay=0, need=0, op=NOTHING):
-    return dict(src=src, dst=dst, w=w, add=add, factor=factor, tanh=tanh, send=send, by=by,
-                recv=recv, relay=relay, need=need, op=op)
+         recv=NONE, relay=0, need=0, op=NOTHING, rsrc=None):
+    if rsrc is None:
+        rsrc = ROUNDED_OF[src] if recv == NONE else recv
+    rdst = ROUNDED_OF.get(dst, UNSENT) if send == UNSENT else send
+    return dict(src=src, dst=dst, w=w, add=add, factor=factor, tanh=tanh, rsrc=rsrc, rdst=rdst,
+                by=by, recv=recv, relay=relay, need=need, op=op)
 
 
 def programs():
@@ -44,29 +51,29 @@
         return step(src, dst, 0, add=RH, factor=WHOLE, **kw)
 
     last = [step(OUT, OUT, 1, op=PUT_1), step(OUT, OUT, 2, op=PUT_2)]
-    body = fine(LEFT) + again()
-    mate = fine(LEFT) + again(RHS)
+    body = fine(TO_LEFT) + again()
+    mate = fine(TO_LEFT) + again(TO_RHS)
     final = [whole(FINAL, LF, relay=1)]
     owner_second = [whole(SECOND, TMP), step(TMP, PSI, 0, factor=WHOLE, op=OWNER)]
     relaxed = [whole(FIRST, TMP, need=1), own(TMP, CC)] + final + [
         step(LF, DUMP, 0, factor=WHOLE, tanh=TT, op=PUT_0)]
     return {
-        "start": fine(LEFT, TT, START) + last,
-        "lead_first": body + [own(LF, CC, tanh=TT, recv=FIRST, send=FIRST, by=BY_TWO, op=PUT_0)] + last,
+        "start": fine(TO_LEFT, TT, START) + last,
+        "lead_first": body + [own(LF, CC, tanh=TT, recv=FIRST, send=TO_FIRST, by=BY_TWO, op=PUT_0)] + last,
         "mate_first": mate + [own(LF, CC, tanh=TT, recv=FIRST, op=PUT_0)] + last,
         "owner_first": body + [
             step(TMP, XZ, 0, factor=FOUR), whole(FIRST, LF, relay=1, need=1),
             own(LF, CC, tanh=TT, op=OWNER_0)] + last,
-        "head": fine(LEFT) + again(RHS, FIRST_POINT) + [
+        "head": fine(TO_LEFT) + again(TO_RHS, FIRST_POINT) + [
             own(LF, CC, tanh=TT, recv=FINAL, op=PUT_0)] + last + [
-            step(LF, XZ, COARSEN, factor=FOUR, need=2),
+            step(LF, XZ, COARSEN, factor=FOUR, need=2, rsrc=FINAL),
             step(TMP, TMP, COARSEN, factor=FOUR, recv=SECOND, op=CHANGES)],
         "lead": body + [
-            own(LF, TMP, recv=FIRST, send=FIRST, by=BY_TWO),
+            own(LF, TMP, recv=FIRST, send=TO_FIRST, by=BY_TWO),
             whole(FINAL, LF, relay=1, need=1),
-            own(LF, CC, tanh=TT, send=FINAL, by=BY_TWO, op=PUT_0),
+            own(LF, CC, tanh=TT, send=TO_FINAL, by=BY_TWO, op=PUT_0),
             whole(SECOND, TMP, relay=1),
-            own(TMP, TMP, send=SECOND, by=BY_TWO)] + last,
+            own(TMP, TMP, send=TO_SECOND, by=BY_TWO)] + last,
         "mate": mate + [own(LF, CC, tanh=TT, recv=FINAL, op=PUT_0)] + last,
         "owner": body + relaxed + owner_second + last,
         "owner_last": body + relaxed + last + owner_second,
@@ -83,7 +90,7 @@
 
 def kernel(
     devices, x_hbm, g_hbm, w_hbm, o_ref,
-    xg, w, pad, st, sent, got,
+    xg, w, st, rounded, part, side_sum, base,
     send_sem, relay_sem, extra_sem, recv_sem, load_sem, weight_sem,
 ):
     f32, bf16 = jnp.float32, jnp.bfloat16
@@ -188,28 +195,41 @@
             device_id={"layer": p + by}, device_id_type=pl.DeviceIdType.MESH,
         )
 
+    def inner(slot):
+        return rounded.at[slot, pl.ds(WIDTH, cells)]
+
+    def landing(slot):
+        return jnp.where(slot == TO_RHS, RHS, slot - (TO_LEFT - LEFT))
+
     def message(i, slot, by):
-        return remote(sent.at[slot], got.at[slot], send_sem.at[i], recv_sem.at[slot], by)
+        to = landing(slot)
+        return remote(inner(slot), inner(to), send_sem.at[i], recv_sem.at[to], by)
 
     def relay_of(i, slot):
-        return remote(got.at[slot], got.at[slot], relay_sem.at[i], recv_sem.at[slot], -1)
+        return remote(inner(slot), inner(slot), relay_sem.at[i], recv_sem.at[slot], -1)
 
     back = jnp.where(p > 0, -1, 1)
 
     def arrived(slot):
-        remote(sent.at[slot], got.at[slot], extra_sem.at[0], recv_sem.at[slot], back).wait_recv()
+        remote(inner(slot), inner(slot), extra_sem.at[0], recv_sem.at[slot], back).wait_recv()
 
     def weight_to(by):
         return remote(w.at[0], w.at[COARSEN], extra_sem.at[0], recv_sem.at[WEIGHT], by)
 
-    def special(n, slot, by):
-        return remote(sent.at[slot], got.at[slot], extra_sem.at[n], recv_sem.at[slot], by)
+    def special(n, slot, to, by):
+        return remote(inner(slot), inner(to), extra_sem.at[n], recv_sem.at[to], by)
+
+    def rounded_store(slot, value):
+        rounded[slot, WIDTH:WIDTH + cells, :] = value.astype(bf16)
 
     def distance(code):
         return jnp.where(code == BY_TWO, 2, 1)
 
-    pad[:, 0:WIDTH, :] = jnp.zeros((3, WIDTH, chans), bf16)
-    pad[:, WIDTH + cells:, :] = jnp.zeros((3, WIDTH, chans), bf16)
+    half = chans // 2
+    rounded[:, 0:WIDTH, :] = jnp.zeros((ROUNDED, WIDTH, chans), bf16)
+    rounded[:, WIDTH + cells:, :] = jnp.zeros((ROUNDED, WIDTH, chans), bf16)
+    part[:, :, 0:8, :] = jnp.zeros((2, 2, 8, half), f32)
+    part[:, :, 8 + cells:, :] = jnp.zeros((2, 2, 8, half), f32)
     st[ZERO] = jnp.zeros((cells, chans), f32)
 
     def put(n):
@@ -219,11 +239,14 @@
     loaded = xg[0].T
     st[LF] = loaded
     st[CP] = loaded
+    rounded_store(CPB, loaded)
 
     @pl.when(first_owner)
     def _():
         start_load.wait()
-        st[TMP] = xg[1].T
+        start = xg[1].T
+        st[TMP] = start
+        rounded_store(TMPB, start)
 
     def finish_owner(xy):
         cc = st[CC]
@@ -232,26 +255,40 @@
 
         @pl.when(lead_next)
         def _():
-            sent[FINAL] = solved.astype(bf16)
-            special(1, FINAL, 2).start()
-            sent[SECOND] = cc.astype(bf16)
-            special(2, SECOND, 2).start()
+            rounded_store(TO_FINAL, solved)
+            special(1, TO_FINAL, FINAL, 2).start()
+            rounded_store(TO_SECOND, cc)
+            special(2, TO_SECOND, SECOND, 2).start()
 
         st[CC] = solved
 
-    def run(i, _):
+    rows_of = cells // BLOCKS
+    col = lax.rem(lax.broadcasted_iota(jnp.int32, (rows_of, chans), 0), WIDTH)
+    order = [
+        [(1, 0), (0, 0), (2, 0), (0, 1), (1, 1)],
+        [(1, 2), (0, 2), (2, 2), (2, 1), (1, 1)],
+    ]
+
+    def push(which, k, m):
+        dy, dx = order[m][k]
+        tap = 3 * dy + dx
+        pltpu.matmul_push_rhs(
+            w[which, :, tap * chans:(tap + 1) * chans], k % 2, m, transpose=True
+        )
+
+    def wait_weights(j):
+        for load in weight_loads(j):
+            load.wait()
+
+    def run(sides, middles, i, _):
         f = {field: entry(field, i) for field in FIELDS}
-        is_fine = i < COARSEN
-
-        @pl.when(is_fine)
-        def _():
-            for load in weight_loads(i):
-                load.wait()
-
-            @pl.when(i < COARSEN - 2)
-            def _():
-                for load in weight_loads(i + 2):
-                    load.start()
+        next_w = entry("w", i + 1)
+        next_need = jnp.where(i + 1 < count, entry("need", i + 1), 0)
+
+        @pl.when(i < COARSEN - 2)
+        def _():
+            for load in weight_loads(i + 2):
+                load.start()
 
         @pl.when(i == 1)
         def _():
@@ -265,16 +302,9 @@
             def _():
                 weight_to(1 - COARSEN).start()
 
-        @pl.when(f["need"] > 0)
-        def _():
-            remote(w.at[0], w.at[COARSEN], extra_sem.at[0], recv_sem.at[WEIGHT], back).wait_recv()
-
-        @pl.when(f["need"] == 1)
-        def _():
-            arrived(RHS)
-            st[RHM] = got[RHS].astype(f32)
-
-        @pl.when(f["recv"] != NONE)
+        received = f["recv"] != NONE
+
+        @pl.when(received)
         def _():
             arrived(f["recv"])
 
@@ -282,31 +312,66 @@
             def _():
                 relay_of(i, f["recv"]).start()
 
-            st[f["src"]] = got[f["recv"]].astype(f32)
-
-        v = st[f["src"]]
-        col = lax.rem(lax.broadcasted_iota(jnp.int32, v.shape, 0), WIDTH)
-        zero = jnp.zeros_like(v)
-        before = jnp.where(col == 0, zero, pltpu.roll(v, 1, 0))
-        after = jnp.where(col == WIDTH - 1, zero, pltpu.roll(v, cells - 1, 0))
-        for d, piece in enumerate((before, v, after)):
-            pad[d, WIDTH:WIDTH + cells, :] = piece.astype(bf16)
-        patches = jnp.concatenate([
-            pad[dx, WIDTH * dy:WIDTH * dy + cells, :] for dy in range(3) for dx in range(3)
-        ], 1)
-        total = lax.dot_general(
-            patches, w[f["w"]], (((1,), (1,)), ((), ())), preferred_element_type=f32,
-        )
-        t = jnp.tanh(total)
+        source = f["rsrc"]
+
+        def lhs(dy, r):
+            return rounded[source, WIDTH * dy + r * rows_of:WIDTH * dy + (r + 1) * rows_of, :]
+
+        for k in range(5):
+            for m in (0, 1):
+                if k < 4:
+                    push(f["w"], k + 1, m)
+            for m in (0, 1):
+                dy = order[m][k][0]
+                total = sides[m] if k < 3 else middles[m]
+                taken = range(BLOCKS) if k < 4 else range(m, BLOCKS, 2)
+                for n, r in enumerate(taken):
+                    pltpu.matmul_acc_lhs(total[r], lhs(dy, r), k % 2 if n == 0 else None)
+        for r in range(BLOCKS):
+            for m in (0, 1):
+                t = pltpu.matmul_pop(sides[m][r])
+                t = jnp.where(col == (0 if m else WIDTH - 1), 0.0, t)
+                for h in (0, 1):
+                    part[m, h, 8 + r * rows_of:8 + (r + 1) * rows_of, :] = t[:, h * half:(h + 1) * half]
+        for r in range(BLOCKS):
+            for h in (0, 1):
+                side_sum[r * rows_of:(r + 1) * rows_of, h * half:(h + 1) * half] = (
+                    part[0, h, 7 + r * rows_of:7 + (r + 1) * rows_of, :]
+                    + part[1, h, 9 + r * rows_of:9 + (r + 1) * rows_of, :]
+                )
+        v = jnp.where(received, rounded[source, WIDTH:WIDTH + cells, :].astype(f32), st[f["src"]])
+        base[...] = v + st[f["add"]]
+        st[f["src"]] = v
+
+        @pl.when(i < COARSEN - 1)
+        def _():
+            wait_weights(i + 1)
+
+        @pl.when(next_need > 0)
+        def _():
+            remote(w.at[0], w.at[COARSEN], extra_sem.at[0], recv_sem.at[WEIGHT], back).wait_recv()
+
+        @pl.when(next_need == 1)
+        def _():
+            arrived(RHS)
+            st[RHM] = rounded[RHS, WIDTH:WIDTH + cells, :].astype(f32)
+
+        for m in (0, 1):
+            push(next_w, 0, m)
         factor = jnp.where(f["factor"] == QUARTER, 0.25, jnp.where(f["factor"] == WHOLE, 1.0, 4.0))
-        new = (st[f["src"]] + factor * t) + st[f["add"]]
-        st[f["tanh"]] = t
-        st[f["dst"]] = new
-        sent[f["send"]] = new.astype(bf16)
-
-        @pl.when(jnp.logical_and(f["send"] != UNSENT, has_next))
-        def _():
-            message(i, f["send"], distance(f["by"])).start()
+        for r in range(BLOCKS):
+            at = slice(r * rows_of, (r + 1) * rows_of)
+            t = jnp.tanh(
+                (pltpu.matmul_pop(middles[0][r]) + pltpu.matmul_pop(middles[1][r])) + side_sum[at]
+            )
+            new = base[at] + factor * t
+            st[f["tanh"], at] = t
+            st[f["dst"], at] = new
+            rounded[f["rdst"], WIDTH + r * rows_of:WIDTH + (r + 1) * rows_of, :] = new.astype(bf16)
+
+        @pl.when(jnp.logical_and(f["rdst"] > UNSENT, has_next))
+        def _():
+            message(i, f["rdst"], distance(f["by"])).start()
 
         op = f["op"]
 
@@ -322,13 +387,13 @@
             rhs = st[CP] + ((st[CP] - psi) - st[CP])
             first = psi + rhs
             st[CC] = first
-            sent[FIRST] = first.astype(bf16)
-            special(1, FIRST, 1).start()
+            rounded_store(TO_FIRST, first)
+            special(1, TO_FIRST, FIRST, 1).start()
 
         @pl.when(op == FIRST_POINT)
         def _():
-            sent[FIRST] = (st[PSI] + st[RH]).astype(bf16)
-            special(1, FIRST, 1).start()
+            rounded_store(TO_FIRST, st[PSI] + st[RH])
+            special(1, TO_FIRST, FIRST, 1).start()
 
         @pl.when(op == OWNER_0)
         def _():
@@ -337,7 +402,9 @@
 
         @pl.when(jnp.logical_or(op == PUT_0, jnp.logical_or(op == START, op == OWNER_0)))
         def _():
-            st[OUT] = st[LF] + 0.25 * st[TT]
+            out = st[LF] + 0.25 * st[TT]
+            st[OUT] = out
+            rounded_store(OUTB, out)
 
         put_at = jnp.where(op == PUT_1, 1, jnp.where(op == PUT_2, 2, 0))
 
@@ -348,23 +415,36 @@
         @pl.when(op == OWNER)
         def _():
             arrived(CHANGE)
-            st[XZ] = got[CHANGE].astype(f32)
+            st[XZ] = rounded[CHANGE, WIDTH:WIDTH + cells, :].astype(f32)
             finish_owner(ZERO)
 
         @pl.when(op == CHANGES)
         def _():
-            sent[CHANGE] = (st[XZ] - st[TMP]).astype(bf16)
-            special(2, CHANGE, COARSEN - 1).start()
+            rounded_store(TO_CHANGE, st[XZ] - st[TMP])
+            special(2, TO_CHANGE, CHANGE, COARSEN - 1).start()
 
         return 0
 
-    lax.fori_loop(0, count, run, 0)
+    def loop(*totals):
+        sides = (totals[:BLOCKS], totals[2 * BLOCKS:3 * BLOCKS])
+        middles = (totals[BLOCKS:2 * BLOCKS], totals[3 * BLOCKS:])
+        wait_weights(0)
+        for m in (0, 1):
+            push(0, 0, m)
+        lax.fori_loop(0, count, functools.partial(run, sides, middles), 0)
+        for m in (0, 1):
+            pltpu.matmul_acc_lhs(sides[m][0], rounded[CPB, 0:rows_of, :], 0)
+            side_sum[0:rows_of, :] = pltpu.matmul_pop(sides[m][0])
+
+    pl.run_scoped(
+        loop, *[pltpu.ACC(m)((rows_of, chans), f32) for m in (0, 1) for _ in range(2 * BLOCKS)]
+    )
     o_ref[COARSEN - 1] = st[CC].T
 
     def drain(i, _):
-        slot = entry("send", i)
-
-        @pl.when(jnp.logical_and(slot != UNSENT, has_next))
+        slot = entry("rdst", i)
+
+        @pl.when(jnp.logical_and(slot > UNSENT, has_next))
         def _():
             message(i, slot, distance(entry("by", i))).wait_send()
 
@@ -382,16 +462,15 @@
             copy.wait_send()
 
     drain_special(weight_to(1), jnp.logical_or(shares, owner_shares))
-    drain_special(special(1, FIRST, 1), phase == 0)
-    drain_special(special(2, CHANGE, COARSEN - 1), changes)
+    drain_special(special(1, TO_FIRST, FIRST, 1), phase == 0)
+    drain_special(special(2, TO_CHANGE, CHANGE, COARSEN - 1), changes)
     sends_solved = jnp.logical_and(owner, lead_next)
-    drain_special(special(1, FINAL, 2), sends_solved)
-    drain_special(special(2, SECOND, 2), sends_solved)
+    drain_special(special(1, TO_FINAL, FINAL, 2), sends_solved)
+    drain_special(special(2, TO_SECOND, SECOND, 2), sends_solved)
 
 
 def per_device(devices, inputs, guess, weights):
     chans, cells = inputs.shape
-    messages = pltpu.VMEM((SLOTS, cells, chans), jnp.bfloat16)
     return pl.pallas_call(
         functools.partial(kernel, devices),
         name="cycle",
@@ -401,13 +480,15 @@
         scratch_shapes=[
             pltpu.VMEM((2, chans, cells), jnp.float32),
             pltpu.VMEM((COARSEN + 1,) + weights.shape[1:], jnp.bfloat16),
-            pltpu.VMEM((3, cells + 2 * WIDTH, chans), jnp.bfloat16),
             pltpu.VMEM((STATES, cells, chans), jnp.float32),
-            messages, messages,
+            pltpu.VMEM((ROUNDED, cells + 2 * WIDTH, chans), jnp.bfloat16),
+            pltpu.VMEM((2, 2, cells + 16, chans // 2), jnp.float32),
+            pltpu.VMEM((cells, chans), jnp.float32),
+            pltpu.VMEM((cells, chans), jnp.float32),
             pltpu.SemaphoreType.DMA((MAX_STEPS,)),
             pltpu.SemaphoreType.DMA((MAX_STEPS,)),
             pltpu.SemaphoreType.DMA((3,)),
-            pltpu.SemaphoreType.DMA((SLOTS + 1,)),
+            pltpu.SemaphoreType.DMA((ROUNDED + 1,)),
             pltpu.SemaphoreType.DMA((2,)),
             pltpu.SemaphoreType.DMA((COARSEN, PIECES)),
         ],

time: 27 us -> 26.7 us (0.989)
  Pallas kernels: 25.9 us -> 25.6 us
    pallas_call x1, Pallas kernels: 25.9 us -> 25.6 us  [per_device(): pl.pallas_call(functools.partial(kernel, devices), name='cycle', out_shap...]
where the time goes in v2:
time: 26.7 us; the launch traced here: 26.5 us
  Pallas kernels  25.6 us (96%)
  local copies, waits for them, and re-layouts  0.97 us (4%)
    pallas_call x1, Pallas kernels, per_device(): pl.pallas_call(functools.partial(kernel, devices), name='cycle', out_shap...  25.6 us
    unnamed x1, local copies, waits for them, and re-layouts  0.97 us

profile of v2, /device:TPU:29, one launch (start us, length us, event | category | flops | bytes accessed | tf_op | source)
XLA Modules:
  0.0 26.5 jit_solution(17398014033004219633)
XLA Ops:
  0.0 25.6 %cycle.1 = f32[4,256,256]{2,1,0:T(8,128)S(1)} custom-call(f32[256,256]{1,0:T(8,128)} %x_hbm.1, f32[1,256,256]{2,1,0:T(8,128)} %g_hbm.1, bf16[4,256,2304]{2,1,0:T(8,128)(2,1)} %w_hbm.1), custom_call_target="tpu_custom_call" | custom-call | tf_op jit(solution)/shard_map/cycle/pallas_call | solution.py:474
  25.6 1.0 %copy.5 = f32[4,256,256]{2,1,0:T(8,128)} copy(f32[4,256,256]{2,1,0:T(8,128)S(1)} %cycle.1) | data formatting | bytes 2097152

commit v3 on v2

--- a/solution.py
+++ b/solution.py
@@ -11,7 +11,6 @@
 COARSEN = 4
 NONE = 15
 PIECES = 8
-MAX_STEPS = 16
 BLOCKS = 4
 ZERO, CP, LF, CC, RH, RHM, TT, PSI, QQ, XZ, OUT, TMP, DUMP = range(13)
 STATES = 13
@@ -19,29 +18,29 @@
 TO_LEFT, TO_FIRST, TO_SECOND, TO_FINAL, TO_CHANGE, TO_RHS, CHANGE, RHS = range(10, 18)
 ROUNDED = 18
 WEIGHT = ROUNDED
-NOTHING, PSI_OF_LEFT, FIRST_POINT, START, PUT_0, PUT_1, PUT_2, OWNER_0, OWNER, CHANGES = range(10)
-FIELDS = ("src", "dst", "w", "add", "factor", "tanh", "rsrc", "rdst", "by", "recv", "relay", "need", "op")
+NOTHING, PSI_OF_LEFT, FIRST_POINT, START, PUT_0, PUT_1, PUT_2, OWNER_0, OWNER, CHANGES, KEEP = range(11)
+FIELDS = ("src", "dst", "w", "add", "factor", "rsrc", "rdst", "by", "recv", "relay", "need", "op")
 BY_ONE, BY_TWO = 0, 1
 QUARTER, WHOLE, FOUR = 0, 1, 2
 ROUNDED_OF = {CP: CPB, LF: LFB, CC: CCB, OUT: OUTB, TMP: TMPB}
 
 
-def step(src, dst, w, add=ZERO, factor=QUARTER, tanh=DUMP, send=UNSENT, by=BY_ONE,
+def step(src, dst, w, add=ZERO, factor=QUARTER, send=UNSENT, by=BY_ONE,
          recv=NONE, relay=0, need=0, op=NOTHING, rsrc=None):
     if rsrc is None:
         rsrc = ROUNDED_OF[src] if recv == NONE else recv
     rdst = ROUNDED_OF.get(dst, UNSENT) if send == UNSENT else send
-    return dict(src=src, dst=dst, w=w, add=add, factor=factor, tanh=tanh, rsrc=rsrc, rdst=rdst,
+    return dict(src=src, dst=dst, w=w, add=add, factor=factor, rsrc=rsrc, rdst=rdst,
                 by=by, recv=recv, relay=relay, need=need, op=op)
 
 
 def programs():
-    def fine(send=UNSENT, tanh=DUMP, op=NOTHING):
-        return [step(CP, CP, 0, tanh=tanh), step(CP, CP, 1), step(CP, CP, 2),
+    def fine(send=UNSENT, first=NOTHING, op=NOTHING):
+        return [step(CP, CP, 0, op=first), step(CP, CP, 1), step(CP, CP, 2),
                 step(CP, CP, 3, send=send, op=op)]
 
     def again(send=UNSENT, op=NOTHING):
-        return [step(LF, CC, 0, tanh=TT, recv=LEFT, op=PSI_OF_LEFT), step(CC, CC, 1),
+        return [step(LF, CC, 0, recv=LEFT, op=PSI_OF_LEFT), step(CC, CC, 1),
                 step(CC, CC, 2), step(CC, RH, 3, add=QQ, send=send, op=op)]
 
     def whole(recv, dst, relay=0, need=0):
@@ -56,25 +55,25 @@
     final = [whole(FINAL, LF, relay=1)]
     owner_second = [whole(SECOND, TMP), step(TMP, PSI, 0, factor=WHOLE, op=OWNER)]
     relaxed = [whole(FIRST, TMP, need=1), own(TMP, CC)] + final + [
-        step(LF, DUMP, 0, factor=WHOLE, tanh=TT, op=PUT_0)]
+        step(LF, DUMP, 0, factor=WHOLE, op=PUT_0)]
     return {
-        "start": fine(TO_LEFT, TT, START) + last,
-        "lead_first": body + [own(LF, CC, tanh=TT, recv=FIRST, send=TO_FIRST, by=BY_TWO, op=PUT_0)] + last,
-        "mate_first": mate + [own(LF, CC, tanh=TT, recv=FIRST, op=PUT_0)] + last,
+        "start": fine(TO_LEFT, KEEP, START) + last,
+        "lead_first": body + [own(LF, CC, recv=FIRST, send=TO_FIRST, by=BY_TWO, op=PUT_0)] + last,
+        "mate_first": mate + [own(LF, CC, recv=FIRST, op=PUT_0)] + last,
         "owner_first": body + [
             step(TMP, XZ, 0, factor=FOUR), whole(FIRST, LF, relay=1, need=1),
-            own(LF, CC, tanh=TT, op=OWNER_0)] + last,
+            own(LF, CC, op=OWNER_0)] + last,
         "head": fine(TO_LEFT) + again(TO_RHS, FIRST_POINT) + [
-            own(LF, CC, tanh=TT, recv=FINAL, op=PUT_0)] + last + [
+            own(LF, CC, recv=FINAL, op=PUT_0)] + last + [
             step(LF, XZ, COARSEN, factor=FOUR, need=2, rsrc=FINAL),
             step(TMP, TMP, COARSEN, factor=FOUR, recv=SECOND, op=CHANGES)],
         "lead": body + [
             own(LF, TMP, recv=FIRST, send=TO_FIRST, by=BY_TWO),
             whole(FINAL, LF, relay=1, need=1),
-            own(LF, CC, tanh=TT, send=TO_FINAL, by=BY_TWO, op=PUT_0),
+            own(LF, CC, send=TO_FINAL, by=BY_TWO, op=PUT_0),
             whole(SECOND, TMP, relay=1),
             own(TMP, TMP, send=TO_SECOND, by=BY_TWO)] + last,
-        "mate": mate + [own(LF, CC, tanh=TT, recv=FINAL, op=PUT_0)] + last,
+        "mate": mate + [own(LF, CC, recv=FINAL, op=PUT_0)] + last,
         "owner": body + relaxed + owner_second + last,
         "owner_last": body + relaxed + last + owner_second,
     }
@@ -125,7 +124,7 @@
     def _():
         own_load.start()
 
-    for load in weight_loads(0) + weight_loads(1):
+    for load in weight_loads(0):
         load.start()
 
     @pl.when(first_owner)
@@ -201,12 +200,12 @@
     def landing(slot):
         return jnp.where(slot == TO_RHS, RHS, slot - (TO_LEFT - LEFT))
 
-    def message(i, slot, by):
+    def message(slot, by):
         to = landing(slot)
-        return remote(inner(slot), inner(to), send_sem.at[i], recv_sem.at[to], by)
-
-    def relay_of(i, slot):
-        return remote(inner(slot), inner(slot), relay_sem.at[i], recv_sem.at[slot], -1)
+        return remote(inner(slot), inner(to), send_sem.at[slot - TO_LEFT], recv_sem.at[to], by)
+
+    def relay_of(slot):
+        return remote(inner(slot), inner(slot), relay_sem.at[slot - LEFT], recv_sem.at[slot], -1)
 
     back = jnp.where(p > 0, -1, 1)
 
@@ -216,8 +215,8 @@
     def weight_to(by):
         return remote(w.at[0], w.at[COARSEN], extra_sem.at[0], recv_sem.at[WEIGHT], by)
 
-    def special(n, slot, to, by):
-        return remote(inner(slot), inner(to), extra_sem.at[n], recv_sem.at[to], by)
+    def special(slot, to, by):
+        return remote(inner(slot), inner(to), send_sem.at[slot - TO_LEFT], recv_sem.at[to], by)
 
     def rounded_store(slot, value):
         rounded[slot, WIDTH:WIDTH + cells, :] = value.astype(bf16)
@@ -236,6 +235,8 @@
         o_ref[n] = st[OUT].T
 
     own_load.wait()
+    for load in weight_loads(1):
+        load.start()
     loaded = xg[0].T
     st[LF] = loaded
     st[CP] = loaded
@@ -256,9 +257,9 @@
         @pl.when(lead_next)
         def _():
             rounded_store(TO_FINAL, solved)
-            special(1, TO_FINAL, FINAL, 2).start()
+            special(TO_FINAL, FINAL, 2).start()
             rounded_store(TO_SECOND, cc)
-            special(2, TO_SECOND, SECOND, 2).start()
+            special(TO_SECOND, SECOND, 2).start()
 
         st[CC] = solved
 
@@ -280,27 +281,30 @@
         for load in weight_loads(j):
             load.wait()
 
-    def run(sides, middles, i, _):
-        f = {field: entry(field, i) for field in FIELDS}
-        next_w = entry("w", i + 1)
-        next_need = jnp.where(i + 1 < count, entry("need", i + 1), 0)
-
-        @pl.when(i < COARSEN - 2)
-        def _():
-            for load in weight_loads(i + 2):
-                load.start()
-
-        @pl.when(i == 1)
-        def _():
-            pl.semaphore_wait(barrier, greeted)
-
-            @pl.when(shares)
-            def _():
-                weight_to(1).start()
-
-            @pl.when(owner_shares)
-            def _():
-                weight_to(1 - COARSEN).start()
+    def fields_of(i):
+        return tuple(entry(field, i) for field in FIELDS)
+
+    def run(sides, middles, i, fields):
+        f = dict(zip(FIELDS, fields))
+
+        @pl.when(i < COARSEN - 1)
+        def _():
+            @pl.when(i < COARSEN - 2)
+            def _():
+                for load in weight_loads(i + 2):
+                    load.start()
+
+            @pl.when(i == 1)
+            def _():
+                pl.semaphore_wait(barrier, greeted)
+
+                @pl.when(shares)
+                def _():
+                    weight_to(1).start()
+
+                @pl.when(owner_shares)
+                def _():
+                    weight_to(1 - COARSEN).start()
 
         received = f["recv"] != NONE
 
@@ -310,7 +314,7 @@
 
             @pl.when(f["relay"] == 1)
             def _():
-                relay_of(i, f["recv"]).start()
+                relay_of(f["recv"]).start()
 
         source = f["rsrc"]
 
@@ -343,21 +347,27 @@
         base[...] = v + st[f["add"]]
         st[f["src"]] = v
 
-        @pl.when(i < COARSEN - 1)
-        def _():
-            wait_weights(i + 1)
-
-        @pl.when(next_need > 0)
-        def _():
-            remote(w.at[0], w.at[COARSEN], extra_sem.at[0], recv_sem.at[WEIGHT], back).wait_recv()
-
-        @pl.when(next_need == 1)
-        def _():
-            arrived(RHS)
-            st[RHM] = rounded[RHS, WIDTH:WIDTH + cells, :].astype(f32)
+        later = fields_of(i + 1)
+        following = dict(zip(FIELDS, later))
+        next_need = jnp.where(i + 1 < count, following["need"], 0)
+
+        @pl.when(jnp.logical_or(i < COARSEN - 1, next_need > 0))
+        def _():
+            @pl.when(i < COARSEN - 1)
+            def _():
+                wait_weights(i + 1)
+
+            @pl.when(next_need > 0)
+            def _():
+                remote(w.at[0], w.at[COARSEN], extra_sem.at[0], recv_sem.at[WEIGHT], back).wait_recv()
+
+            @pl.when(next_need == 1)
+            def _():
+                arrived(RHS)
+                st[RHM] = rounded[RHS, WIDTH:WIDTH + cells, :].astype(f32)
 
         for m in (0, 1):
-            push(next_w, 0, m)
+            push(following["w"], 0, m)
         factor = jnp.where(f["factor"] == QUARTER, 0.25, jnp.where(f["factor"] == WHOLE, 1.0, 4.0))
         for r in range(BLOCKS):
             at = slice(r * rows_of, (r + 1) * rows_of)
@@ -365,65 +375,73 @@
                 (pltpu.matmul_pop(middles[0][r]) + pltpu.matmul_pop(middles[1][r])) + side_sum[at]
             )
             new = base[at] + factor * t
-            st[f["tanh"], at] = t
             st[f["dst"], at] = new
             rounded[f["rdst"], WIDTH + r * rows_of:WIDTH + (r + 1) * rows_of, :] = new.astype(bf16)
 
         @pl.when(jnp.logical_and(f["rdst"] > UNSENT, has_next))
         def _():
-            message(i, f["rdst"], distance(f["by"])).start()
+            message(f["rdst"], distance(f["by"])).start()
 
         op = f["op"]
 
-        @pl.when(op == PSI_OF_LEFT)
-        def _():
-            psi = st[LF] + st[TT]
-            st[PSI] = psi
-            st[QQ] = (st[CP] - psi) - st[CP]
-
-        @pl.when(op == START)
-        def _():
-            psi = st[LF] + st[TT]
-            rhs = st[CP] + ((st[CP] - psi) - st[CP])
-            first = psi + rhs
-            st[CC] = first
-            rounded_store(TO_FIRST, first)
-            special(1, TO_FIRST, FIRST, 1).start()
-
-        @pl.when(op == FIRST_POINT)
-        def _():
-            rounded_store(TO_FIRST, st[PSI] + st[RH])
-            special(1, TO_FIRST, FIRST, 1).start()
-
-        @pl.when(op == OWNER_0)
-        def _():
-            st[PSI] = st[LF] + st[TT]
-            finish_owner(XZ)
-
-        @pl.when(jnp.logical_or(op == PUT_0, jnp.logical_or(op == START, op == OWNER_0)))
-        def _():
-            out = st[LF] + 0.25 * st[TT]
-            st[OUT] = out
-            rounded_store(OUTB, out)
-
-        put_at = jnp.where(op == PUT_1, 1, jnp.where(op == PUT_2, 2, 0))
-
-        @pl.when(jnp.logical_and(op >= START, op <= OWNER_0))
-        def _():
-            put(put_at)
-
-        @pl.when(op == OWNER)
-        def _():
-            arrived(CHANGE)
-            st[XZ] = rounded[CHANGE, WIDTH:WIDTH + cells, :].astype(f32)
-            finish_owner(ZERO)
-
-        @pl.when(op == CHANGES)
-        def _():
-            rounded_store(TO_CHANGE, st[XZ] - st[TMP])
-            special(2, TO_CHANGE, CHANGE, COARSEN - 1).start()
-
-        return 0
+        @pl.when(op != NOTHING)
+        def _():
+            @pl.when(op == PSI_OF_LEFT)
+            def _():
+                psi = st[LF] + 4.0 * (st[CC] - base[...])
+                st[PSI] = psi
+                st[QQ] = (st[CP] - psi) - st[CP]
+
+            @pl.when(op == KEEP)
+            def _():
+                st[TT] = 4.0 * (st[CP] - base[...])
+
+            @pl.when(op == START)
+            def _():
+                psi = st[LF] + st[TT]
+                rhs = st[CP] + ((st[CP] - psi) - st[CP])
+                first = psi + rhs
+                st[CC] = first
+                rounded_store(TO_FIRST, first)
+                special(TO_FIRST, FIRST, 1).start()
+
+            @pl.when(op == FIRST_POINT)
+            def _():
+                rounded_store(TO_FIRST, st[PSI] + st[RH])
+                special(TO_FIRST, FIRST, 1).start()
+
+            @pl.when(op == OWNER_0)
+            def _():
+                t = st[CC] - base[...]
+                st[TT] = t
+                st[PSI] = st[LF] + t
+                finish_owner(XZ)
+
+            @pl.when(jnp.logical_or(op == PUT_0, jnp.logical_or(op == START, op == OWNER_0)))
+            def _():
+                t = jnp.where(op == PUT_0, st[f["dst"]] - base[...], st[TT])
+                out = st[LF] + 0.25 * t
+                st[OUT] = out
+                rounded_store(OUTB, out)
+
+            put_at = jnp.where(op == PUT_1, 1, jnp.where(op == PUT_2, 2, 0))
+
+            @pl.when(jnp.logical_and(op >= START, op <= OWNER_0))
+            def _():
+                put(put_at)
+
+            @pl.when(op == OWNER)
+            def _():
+                arrived(CHANGE)
+                st[XZ] = rounded[CHANGE, WIDTH:WIDTH + cells, :].astype(f32)
+                finish_owner(ZERO)
+
+            @pl.when(op == CHANGES)
+            def _():
+                rounded_store(TO_CHANGE, st[XZ] - st[TMP])
+                special(TO_CHANGE, CHANGE, COARSEN - 1).start()
+
+        return later
 
     def loop(*totals):
         sides = (totals[:BLOCKS], totals[2 * BLOCKS:3 * BLOCKS])
@@ -431,7 +449,7 @@
         wait_weights(0)
         for m in (0, 1):
             push(0, 0, m)
-        lax.fori_loop(0, count, functools.partial(run, sides, middles), 0)
+        lax.fori_loop(0, count, functools.partial(run, sides, middles), fields_of(0))
         for m in (0, 1):
             pltpu.matmul_acc_lhs(sides[m][0], rounded[CPB, 0:rows_of, :], 0)
             side_sum[0:rows_of, :] = pltpu.matmul_pop(sides[m][0])
@@ -441,32 +459,24 @@
     )
     o_ref[COARSEN - 1] = st[CC].T
 
-    def drain(i, _):
-        slot = entry("rdst", i)
-
-        @pl.when(jnp.logical_and(slot > UNSENT, has_next))
-        def _():
-            message(i, slot, distance(entry("by", i))).wait_send()
-
-        @pl.when(entry("relay", i) == 1)
-        def _():
-            relay_of(i, entry("recv", i)).wait_send()
-
-        return 0
-
-    lax.fori_loop(0, count, drain, 0)
-
-    def drain_special(copy, cond):
+    def drain(copy, cond):
         @pl.when(cond)
         def _():
             copy.wait_send()
 
-    drain_special(weight_to(1), jnp.logical_or(shares, owner_shares))
-    drain_special(special(1, TO_FIRST, FIRST, 1), phase == 0)
-    drain_special(special(2, TO_CHANGE, CHANGE, COARSEN - 1), changes)
-    sends_solved = jnp.logical_and(owner, lead_next)
-    drain_special(special(1, TO_FINAL, FINAL, 2), sends_solved)
-    drain_special(special(2, TO_SECOND, SECOND, 2), sends_solved)
+    relaxed = jnp.logical_or(
+        jnp.logical_and(owner, lead_next), jnp.logical_and(phase == 1, group > 0)
+    )
+    drain(weight_to(back), jnp.logical_or(shares, owner_shares))
+    drain(special(TO_LEFT, LEFT, back), has_next)
+    drain(special(TO_RHS, RHS, back), shares)
+    drain(special(TO_FIRST, FIRST, back), phase < 2)
+    drain(special(TO_FINAL, FINAL, back), relaxed)
+    drain(special(TO_SECOND, SECOND, back), relaxed)
+    drain(special(TO_CHANGE, CHANGE, back), changes)
+    drain(relay_of(FIRST), first_owner)
+    drain(relay_of(FINAL), jnp.logical_and(lead, group > 0))
+    drain(relay_of(SECOND), jnp.logical_and(phase == 1, group > 0))
 
 
 def per_device(devices, inputs, guess, weights):
@@ -485,9 +495,9 @@
             pltpu.VMEM((2, 2, cells + 16, chans // 2), jnp.float32),
             pltpu.VMEM((cells, chans), jnp.float32),
             pltpu.VMEM((cells, chans), jnp.float32),
-            pltpu.SemaphoreType.DMA((MAX_STEPS,)),
-            pltpu.SemaphoreType.DMA((MAX_STEPS,)),
-            pltpu.SemaphoreType.DMA((3,)),
+            pltpu.SemaphoreType.DMA((TO_RHS - TO_LEFT + 1,)),
+            pltpu.SemaphoreType.DMA((FINAL - LEFT + 1,)),
+            pltpu.SemaphoreType.DMA((1,)),
             pltpu.SemaphoreType.DMA((ROUNDED + 1,)),
             pltpu.SemaphoreType.DMA((2,)),
             pltpu.SemaphoreType.DMA((COARSEN, PIECES)),

time: 26.7 us -> 26.1 us (0.978)
  Pallas kernels: 25.6 us -> 24.9 us
    pallas_call x1, Pallas kernels: 25.6 us -> 24.9 us  [per_device(): pl.pallas_call(functools.partial(kernel, devices), name='cycle', out_shap...]
where the time goes in v3:
time: 26.1 us; the launch traced here: 25.9 us
  Pallas kernels  24.9 us (95%)
  local copies, waits for them, and re-layouts  0.97 us (4%)
    pallas_call x1, Pallas kernels, per_device(): pl.pallas_call(functools.partial(kernel, devices), name='cycle', out_shap...  24.9 us
    unnamed x1, local copies, waits for them, and re-layouts  0.97 us

profile of v3, /device:TPU:29, one launch (start us, length us, event | category | flops | bytes accessed | tf_op | source)
XLA Modules:
  0.0 25.9 jit_solution(11798718596188475344)
XLA Ops:
  0.0 24.9 %cycle.1 = f32[4,256,256]{2,1,0:T(8,128)S(1)} custom-call(f32[256,256]{1,0:T(8,128)} %x_hbm.1, f32[1,256,256]{2,1,0:T(8,128)} %g_hbm.1, bf16[4,256,2304]{2,1,0:T(8,128)(2,1)} %w_hbm.1), custom_call_target="tpu_custom_call" | custom-call | tf_op jit(solution)/shard_map/cycle/pallas_call | solution.py:484
  24.9 1.0 %copy.5 = f32[4,256,256]{2,1,0:T(8,128)} copy(f32[4,256,256]{2,1,0:T(8,128)S(1)} %cycle.1) | data formatting | bytes 2097152

commit v4 on v3

--- a/solution.py
+++ b/solution.py
@@ -10,7 +10,7 @@
 WIDTH = 16
 COARSEN = 4
 NONE = 15
-PIECES = 8
+PIECES = 2
 BLOCKS = 4
 ZERO, CP, LF, CC, RH, RHM, TT, PSI, QQ, XZ, OUT, TMP, DUMP = range(13)
 STATES = 13
@@ -124,7 +124,7 @@
     def _():
         own_load.start()
 
-    for load in weight_loads(0):
+    for load in weight_loads(0) + weight_loads(1):
         load.start()
 
     @pl.when(first_owner)
@@ -235,7 +235,7 @@
         o_ref[n] = st[OUT].T
 
     own_load.wait()
-    for load in weight_loads(1):
+    for load in weight_loads(2):
         load.start()
     loaded = xg[0].T
     st[LF] = loaded
@@ -287,24 +287,17 @@
     def run(sides, middles, i, fields):
         f = dict(zip(FIELDS, fields))
 
-        @pl.when(i < COARSEN - 1)
-        def _():
-            @pl.when(i < COARSEN - 2)
-            def _():
-                for load in weight_loads(i + 2):
-                    load.start()
-
-            @pl.when(i == 1)
-            def _():
-                pl.semaphore_wait(barrier, greeted)
-
-                @pl.when(shares)
-                def _():
-                    weight_to(1).start()
-
-                @pl.when(owner_shares)
-                def _():
-                    weight_to(1 - COARSEN).start()
+        @pl.when(i == 1)
+        def _():
+            pl.semaphore_wait(barrier, greeted)
+
+            @pl.when(shares)
+            def _():
+                weight_to(1).start()
+
+            @pl.when(owner_shares)
+            def _():
+                weight_to(1 - COARSEN).start()
 
         received = f["recv"] != NONE
 
@@ -321,16 +314,43 @@
         def lhs(dy, r):
             return rounded[source, WIDTH * dy + r * rows_of:WIDTH * dy + (r + 1) * rows_of, :]
 
-        for k in range(5):
-            for m in (0, 1):
-                if k < 4:
-                    push(f["w"], k + 1, m)
+        def stream(k):
             for m in (0, 1):
                 dy = order[m][k][0]
                 total = sides[m] if k < 3 else middles[m]
                 taken = range(BLOCKS) if k < 4 else range(m, BLOCKS, 2)
                 for n, r in enumerate(taken):
                     pltpu.matmul_acc_lhs(total[r], lhs(dy, r), k % 2 if n == 0 else None)
+
+        for m in (0, 1):
+            push(f["w"], 1, m)
+        stream(0)
+        later = fields_of(i + 1)
+        following = dict(zip(FIELDS, later))
+        next_weight = jnp.logical_and(i + 1 < count, following["need"] > 0)
+
+        @pl.when(jnp.logical_or(i < COARSEN - 1, jnp.logical_or(next_weight, f["need"] > 0)))
+        def _():
+            @pl.when(i < COARSEN - 1)
+            def _():
+                wait_weights(i + 1)
+
+            @pl.when(next_weight)
+            def _():
+                remote(w.at[0], w.at[COARSEN], extra_sem.at[0], recv_sem.at[WEIGHT], back).wait_recv()
+
+            @pl.when(f["need"] == 1)
+            def _():
+                arrived(RHS)
+                st[RHM] = rounded[RHS, WIDTH:WIDTH + cells, :].astype(f32)
+
+        for k in range(1, 5):
+            for m in (0, 1):
+                if k < 4:
+                    push(f["w"], k + 1, m)
+            stream(k)
+        for m in (0, 1):
+            push(following["w"], 0, m)
         for r in range(BLOCKS):
             for m in (0, 1):
                 t = pltpu.matmul_pop(sides[m][r])
@@ -347,27 +367,6 @@
         base[...] = v + st[f["add"]]
         st[f["src"]] = v
 
-        later = fields_of(i + 1)
-        following = dict(zip(FIELDS, later))
-        next_need = jnp.where(i + 1 < count, following["need"], 0)
-
-        @pl.when(jnp.logical_or(i < COARSEN - 1, next_need > 0))
-        def _():
-            @pl.when(i < COARSEN - 1)
-            def _():
-                wait_weights(i + 1)
-
-            @pl.when(next_need > 0)
-            def _():
-                remote(w.at[0], w.at[COARSEN], extra_sem.at[0], recv_sem.at[WEIGHT], back).wait_recv()
-
-            @pl.when(next_need == 1)
-            def _():
-                arrived(RHS)
-                st[RHM] = rounded[RHS, WIDTH:WIDTH + cells, :].astype(f32)
-
-        for m in (0, 1):
-            push(following["w"], 0, m)
         factor = jnp.where(f["factor"] == QUARTER, 0.25, jnp.where(f["factor"] == WHOLE, 1.0, 4.0))
         for r in range(BLOCKS):
             at = slice(r * rows_of, (r + 1) * rows_of)
@@ -447,6 +446,8 @@
         sides = (totals[:BLOCKS], totals[2 * BLOCKS:3 * BLOCKS])
         middles = (totals[BLOCKS:2 * BLOCKS], totals[3 * BLOCKS:])
         wait_weights(0)
+        for load in weight_loads(3):
+            load.start()
         for m in (0, 1):
             push(0, 0, m)
         lax.fori_loop(0, count, functools.partial(run, sides, middles), fields_of(0))

time: 26.1 us -> 24.9 us (0.954)
  Pallas kernels: 24.9 us -> 23.8 us
    pallas_call x1, Pallas kernels: 24.9 us -> 23.8 us  [per_device(): pl.pallas_call(functools.partial(kernel, devices), name='cycle', out_shap...]
where the time goes in v4:
time: 24.9 us; the launch traced here: 24.7 us
  Pallas kernels  23.8 us (96%)
  local copies, waits for them, and re-layouts  0.97 us (4%)
    pallas_call x1, Pallas kernels, per_device(): pl.pallas_call(functools.partial(kernel, devices), name='cycle', out_shap...  23.8 us
    unnamed x1, local copies, waits for them, and re-layouts  0.97 us

profile of v4, /device:TPU:29, one launch (start us, length us, event | category | flops | bytes accessed | tf_op | source)
XLA Modules:
  0.0 24.7 jit_solution(13202205235394628136)
XLA Ops:
  0.0 23.8 %cycle.1 = f32[4,256,256]{2,1,0:T(8,128)S(1)} custom-call(f32[256,256]{1,0:T(8,128)} %x_hbm.1, f32[1,256,256]{2,1,0:T(8,128)} %g_hbm.1, bf16[4,256,2304]{2,1,0:T(8,128)(2,1)} %w_hbm.1), custom_call_target="tpu_custom_call" | custom-call | tf_op jit(solution)/shard_map/cycle/pallas_call | solution.py:485
  23.8 1.0 %copy.5 = f32[4,256,256]{2,1,0:T(8,128)} copy(f32[4,256,256]{2,1,0:T(8,128)S(1)} %cycle.1) | data formatting | bytes 2097152

commit v5 on v4

--- a/solution.py
+++ b/solution.py
@@ -12,13 +12,14 @@
 NONE = 15
 PIECES = 2
 BLOCKS = 4
+ROWS = 32
 ZERO, CP, LF, CC, RH, RHM, TT, PSI, QQ, XZ, OUT, TMP, DUMP = range(13)
 STATES = 13
 CPB, LFB, OUTB, CCB, TMPB, LEFT, FIRST, SECOND, FINAL, UNSENT = range(10)
 TO_LEFT, TO_FIRST, TO_SECOND, TO_FINAL, TO_CHANGE, TO_RHS, CHANGE, RHS = range(10, 18)
 ROUNDED = 18
 WEIGHT = ROUNDED
-NOTHING, PSI_OF_LEFT, FIRST_POINT, START, PUT_0, PUT_1, PUT_2, OWNER_0, OWNER, CHANGES, KEEP = range(11)
+NOTHING, PSI_OF_LEFT, FIRST_POINT, CHANGES, KEEP, START, PUT_0, OWNER_0, PUT_1, PUT_2, PUT_LAST, OWNER = range(12)
 FIELDS = ("src", "dst", "w", "add", "factor", "rsrc", "rdst", "by", "recv", "relay", "need", "op")
 BY_ONE, BY_TWO = 0, 1
 QUARTER, WHOLE, FOUR = 0, 1, 2
@@ -49,7 +50,8 @@
     def own(src, dst, **kw):
         return step(src, dst, 0, add=RH, factor=WHOLE, **kw)
 
-    last = [step(OUT, OUT, 1, op=PUT_1), step(OUT, OUT, 2, op=PUT_2)]
+    last = [step(OUT, OUT, 1, op=PUT_1), step(OUT, OUT, 2, op=PUT_LAST)]
+    early = [step(OUT, OUT, 1, op=PUT_1), step(OUT, OUT, 2, op=PUT_2)]
     body = fine(TO_LEFT) + again()
     mate = fine(TO_LEFT) + again(TO_RHS)
     final = [whole(FINAL, LF, relay=1)]
@@ -75,7 +77,7 @@
             own(TMP, TMP, send=TO_SECOND, by=BY_TWO)] + last,
         "mate": mate + [own(LF, CC, recv=FINAL, op=PUT_0)] + last,
         "owner": body + relaxed + owner_second + last,
-        "owner_last": body + relaxed + last + owner_second,
+        "owner_last": body + relaxed + early + owner_second,
     }
 
 
@@ -231,8 +233,16 @@
     part[:, :, 8 + cells:, :] = jnp.zeros((2, 2, 8, half), f32)
     st[ZERO] = jnp.zeros((cells, chans), f32)
 
-    def put(n):
-        o_ref[n] = st[OUT].T
+    def put(slot, n):
+        o_ref[n] = st[slot].T
+
+    def by_rows(body):
+        def rows(r, _):
+            first = pl.multiple_of(r * ROWS, ROWS)
+            body(pl.ds(first, ROWS), pl.ds(WIDTH + first, ROWS))
+            return 0
+
+        lax.fori_loop(0, cells // ROWS, rows, 0)
 
     own_load.wait()
     for load in weight_loads(2):
@@ -249,19 +259,19 @@
         st[TMP] = start
         rounded_store(TMPB, start)
 
-    def finish_owner(xy):
-        cc = st[CC]
-        second = st[RH] - (cc - st[PSI])
-        solved = st[XZ] + ((cc - st[xy]) + second)
-
+    def send_solved():
         @pl.when(lead_next)
         def _():
-            rounded_store(TO_FINAL, solved)
             special(TO_FINAL, FINAL, 2).start()
-            rounded_store(TO_SECOND, cc)
             special(TO_SECOND, SECOND, 2).start()
 
-        st[CC] = solved
+    def solve(at, inner_at, psi, xz, xy):
+        cc = st[CC, at]
+        second = st[RH, at] - (cc - psi)
+        solved = xz + ((cc - xy) + second)
+        rounded[TO_FINAL, inner_at] = solved.astype(bf16)
+        rounded[TO_SECOND, inner_at] = cc.astype(bf16)
+        st[CC, at] = solved
 
     rows_of = cells // BLOCKS
     col = lax.rem(lax.broadcasted_iota(jnp.int32, (rows_of, chans), 0), WIDTH)
@@ -387,57 +397,92 @@
         def _():
             @pl.when(op == PSI_OF_LEFT)
             def _():
-                psi = st[LF] + 4.0 * (st[CC] - base[...])
-                st[PSI] = psi
-                st[QQ] = (st[CP] - psi) - st[CP]
+                def rows(at, _):
+                    psi = st[LF, at] + 4.0 * (st[CC, at] - base[at])
+                    st[PSI, at] = psi
+                    st[QQ, at] = (st[CP, at] - psi) - st[CP, at]
+
+                by_rows(rows)
 
             @pl.when(op == KEEP)
             def _():
-                st[TT] = 4.0 * (st[CP] - base[...])
+                def rows(at, _):
+                    st[TT, at] = 4.0 * (st[CP, at] - base[at])
+
+                by_rows(rows)
 
             @pl.when(op == START)
             def _():
-                psi = st[LF] + st[TT]
-                rhs = st[CP] + ((st[CP] - psi) - st[CP])
-                first = psi + rhs
-                st[CC] = first
-                rounded_store(TO_FIRST, first)
+                def rows(at, inner_at):
+                    psi = st[LF, at] + st[TT, at]
+                    rhs = st[CP, at] + ((st[CP, at] - psi) - st[CP, at])
+                    first = psi + rhs
+                    st[CC, at] = first
+                    rounded[TO_FIRST, inner_at] = first.astype(bf16)
+
+                by_rows(rows)
                 special(TO_FIRST, FIRST, 1).start()
 
             @pl.when(op == FIRST_POINT)
             def _():
-                rounded_store(TO_FIRST, st[PSI] + st[RH])
+                def rows(at, inner_at):
+                    rounded[TO_FIRST, inner_at] = (st[PSI, at] + st[RH, at]).astype(bf16)
+
+                by_rows(rows)
                 special(TO_FIRST, FIRST, 1).start()
 
             @pl.when(op == OWNER_0)
             def _():
-                t = st[CC] - base[...]
-                st[TT] = t
-                st[PSI] = st[LF] + t
-                finish_owner(XZ)
-
-            @pl.when(jnp.logical_or(op == PUT_0, jnp.logical_or(op == START, op == OWNER_0)))
-            def _():
-                t = jnp.where(op == PUT_0, st[f["dst"]] - base[...], st[TT])
-                out = st[LF] + 0.25 * t
-                st[OUT] = out
-                rounded_store(OUTB, out)
-
-            put_at = jnp.where(op == PUT_1, 1, jnp.where(op == PUT_2, 2, 0))
+                def rows(at, inner_at):
+                    t = st[CC, at] - base[at]
+                    st[TT, at] = t
+                    solve(at, inner_at, st[LF, at] + t, st[XZ, at], st[XZ, at])
+
+                by_rows(rows)
+                send_solved()
 
             @pl.when(jnp.logical_and(op >= START, op <= OWNER_0))
             def _():
-                put(put_at)
+                def rows(at, inner_at):
+                    t = jnp.where(op == PUT_0, st[f["dst"], at] - base[at], st[TT, at])
+                    out = st[LF, at] + 0.25 * t
+                    st[OUT, at] = out
+                    rounded[OUTB, inner_at] = out.astype(bf16)
+
+                by_rows(rows)
 
             @pl.when(op == OWNER)
             def _():
                 arrived(CHANGE)
-                st[XZ] = rounded[CHANGE, WIDTH:WIDTH + cells, :].astype(f32)
-                finish_owner(ZERO)
+
+                def rows(at, inner_at):
+                    change = rounded[CHANGE, inner_at].astype(f32)
+                    solve(at, inner_at, st[PSI, at], change, st[ZERO, at])
+
+                by_rows(rows)
+                send_solved()
+
+            @pl.when(op >= START)
+            def _():
+                whole_put = op == OWNER
+
+                def one(n, _):
+                    put_last = jnp.logical_or(whole_put, n == 1)
+                    place = jnp.where(op >= PUT_1, op - PUT_1 + 1, 0)
+                    put(
+                        jnp.where(put_last, CC, OUT),
+                        jnp.where(put_last, COARSEN - 1, jnp.minimum(place, COARSEN - 2)),
+                    )
+                    return 0
+
+                lax.fori_loop(0, jnp.where(op == PUT_LAST, 2, 1), one, 0)
 
             @pl.when(op == CHANGES)
             def _():
-                rounded_store(TO_CHANGE, st[XZ] - st[TMP])
+                def rows(at, inner_at):
+                    rounded[TO_CHANGE, inner_at] = (st[XZ, at] - st[TMP, at]).astype(bf16)
+
+                by_rows(rows)
                 special(TO_CHANGE, CHANGE, COARSEN - 1).start()
 
         return later
@@ -458,7 +503,6 @@
     pl.run_scoped(
         loop, *[pltpu.ACC(m)((rows_of, chans), f32) for m in (0, 1) for _ in range(2 * BLOCKS)]
     )
-    o_ref[COARSEN - 1] = st[CC].T
 
     def drain(copy, cond):
         @pl.when(cond)

time: 24.9 us -> 25.1 us (level)
  no operation moved by 1% of the time
where the time goes in v5:
time: 25.1 us; the launch traced here: 24.9 us
  Pallas kernels  23.9 us (95%)
  local copies, waits for them, and re-layouts  0.97 us (4%)
    pallas_call x1, Pallas kernels, per_device(): pl.pallas_call(functools.partial(kernel, devices), name='cycle', out_shap...  23.9 us
    unnamed x1, local copies, waits for them, and re-layouts  0.97 us

profile of v5, /device:TPU:29, one launch (start us, length us, event | category | flops | bytes accessed | tf_op | source)
XLA Modules:
  0.0 24.9 jit_solution(14027942772419763704)
XLA Ops:
  0.0 23.9 %cycle.1 = f32[4,256,256]{2,1,0:T(8,128)S(1)} custom-call(f32[256,256]{1,0:T(8,128)} %x_hbm.1, f32[1,256,256]{2,1,0:T(8,128)} %g_hbm.1, bf16[4,256,2304]{2,1,0:T(8,128)(2,1)} %w_hbm.1), custom_call_target="tpu_custom_call" | custom-call | tf_op jit(solution)/shard_map/cycle/pallas_call | solution.py:529
  23.9 1.0 %copy.5 = f32[4,256,256]{2,1,0:T(8,128)} copy(f32[4,256,256]{2,1,0:T(8,128)S(1)} %cycle.1) | data formatting | bytes 2097152

commit v6 on v4

--- a/solution.py
+++ b/solution.py
@@ -11,7 +11,7 @@
 COARSEN = 4
 NONE = 15
 PIECES = 2
-BLOCKS = 4
+BLOCKS = 8
 ZERO, CP, LF, CC, RH, RHM, TT, PSI, QQ, XZ, OUT, TMP, DUMP = range(13)
 STATES = 13
 CPB, LFB, OUTB, CCB, TMPB, LEFT, FIRST, SECOND, FINAL, UNSENT = range(10)
@@ -329,6 +329,10 @@
         following = dict(zip(FIELDS, later))
         next_weight = jnp.logical_and(i + 1 < count, following["need"] > 0)
 
+        @pl.when(received)
+        def _():
+            st[f["src"]] = rounded[source, WIDTH:WIDTH + cells, :].astype(f32)
+
         @pl.when(jnp.logical_or(i < COARSEN - 1, jnp.logical_or(next_weight, f["need"] > 0)))
         def _():
             @pl.when(i < COARSEN - 1)
@@ -357,23 +361,17 @@
                 t = jnp.where(col == (0 if m else WIDTH - 1), 0.0, t)
                 for h in (0, 1):
                     part[m, h, 8 + r * rows_of:8 + (r + 1) * rows_of, :] = t[:, h * half:(h + 1) * half]
-        for r in range(BLOCKS):
-            for h in (0, 1):
-                side_sum[r * rows_of:(r + 1) * rows_of, h * half:(h + 1) * half] = (
-                    part[0, h, 7 + r * rows_of:7 + (r + 1) * rows_of, :]
-                    + part[1, h, 9 + r * rows_of:9 + (r + 1) * rows_of, :]
-                )
-        v = jnp.where(received, rounded[source, WIDTH:WIDTH + cells, :].astype(f32), st[f["src"]])
-        base[...] = v + st[f["add"]]
-        st[f["src"]] = v
+        base[...] = st[f["src"]] + st[f["add"]]
 
         factor = jnp.where(f["factor"] == QUARTER, 0.25, jnp.where(f["factor"] == WHOLE, 1.0, 4.0))
         for r in range(BLOCKS):
             at = slice(r * rows_of, (r + 1) * rows_of)
-            t = jnp.tanh(
-                (pltpu.matmul_pop(middles[0][r]) + pltpu.matmul_pop(middles[1][r])) + side_sum[at]
-            )
-            new = base[at] + factor * t
+            middle = pltpu.matmul_pop(middles[0][r]) + pltpu.matmul_pop(middles[1][r])
+            side = jnp.concatenate([
+                part[0, h, 7 + r * rows_of:7 + (r + 1) * rows_of, :]
+                + part[1, h, 9 + r * rows_of:9 + (r + 1) * rows_of, :] for h in (0, 1)
+            ], 1)
+            new = base[at] + factor * jnp.tanh(middle + side)
             st[f["dst"], at] = new
             rounded[f["rdst"], WIDTH + r * rows_of:WIDTH + (r + 1) * rows_of, :] = new.astype(bf16)
 

time: 24.9 us -> 24.2 us (0.972)
  Pallas kernels: 23.8 us -> 23 us
    pallas_call x1, Pallas kernels: 23.8 us -> 23 us  [per_device(): pl.pallas_call(functools.partial(kernel, devices), name='cycle', out_shap...]
where the time goes in v6:
time: 24.2 us; the launch traced here: 24 us
  Pallas kernels  23 us (95%)
  local copies, waits for them, and re-layouts  0.97 us (4%)
    pallas_call x1, Pallas kernels, per_device(): pl.pallas_call(functools.partial(kernel, devices), name='cycle', out_shap...  23 us
    unnamed x1, local copies, waits for them, and re-layouts  0.97 us

profile of v6, /device:TPU:29, one launch (start us, length us, event | category | flops | bytes accessed | tf_op | source)
XLA Modules:
  0.0 24.0 jit_solution(2509533554776957100)
XLA Ops:
  0.0 23.0 %cycle.1 = f32[4,256,256]{2,1,0:T(8,128)S(1)} custom-call(f32[256,256]{1,0:T(8,128)} %x_hbm.1, f32[1,256,256]{2,1,0:T(8,128)} %g_hbm.1, bf16[4,256,2304]{2,1,0:T(8,128)(2,1)} %w_hbm.1), custom_call_target="tpu_custom_call" | custom-call | tf_op jit(solution)/shard_map/cycle/pallas_call | solution.py:483
  23.0 1.0 %copy.5 = f32[4,256,256]{2,1,0:T(8,128)} copy(f32[4,256,256]{2,1,0:T(8,128)S(1)} %cycle.1) | data formatting | bytes 2097152

commit v7 on v5

--- a/solution.py
+++ b/solution.py
@@ -11,8 +11,8 @@
 COARSEN = 4
 NONE = 15
 PIECES = 2
-BLOCKS = 4
-ROWS = 32
+BLOCKS = 8
+ROWS = 128
 ZERO, CP, LF, CC, RH, RHM, TT, PSI, QQ, XZ, OUT, TMP, DUMP = range(13)
 STATES = 13
 CPB, LFB, OUTB, CCB, TMPB, LEFT, FIRST, SECOND, FINAL, UNSENT = range(10)
@@ -339,6 +339,10 @@
         following = dict(zip(FIELDS, later))
         next_weight = jnp.logical_and(i + 1 < count, following["need"] > 0)
 
+        @pl.when(received)
+        def _():
+            st[f["src"]] = rounded[source, WIDTH:WIDTH + cells, :].astype(f32)
+
         @pl.when(jnp.logical_or(i < COARSEN - 1, jnp.logical_or(next_weight, f["need"] > 0)))
         def _():
             @pl.when(i < COARSEN - 1)
@@ -367,23 +371,17 @@
                 t = jnp.where(col == (0 if m else WIDTH - 1), 0.0, t)
                 for h in (0, 1):
                     part[m, h, 8 + r * rows_of:8 + (r + 1) * rows_of, :] = t[:, h * half:(h + 1) * half]
-        for r in range(BLOCKS):
-            for h in (0, 1):
-                side_sum[r * rows_of:(r + 1) * rows_of, h * half:(h + 1) * half] = (
-                    part[0, h, 7 + r * rows_of:7 + (r + 1) * rows_of, :]
-                    + part[1, h, 9 + r * rows_of:9 + (r + 1) * rows_of, :]
-                )
-        v = jnp.where(received, rounded[source, WIDTH:WIDTH + cells, :].astype(f32), st[f["src"]])
-        base[...] = v + st[f["add"]]
-        st[f["src"]] = v
+        base[...] = st[f["src"]] + st[f["add"]]
 
         factor = jnp.where(f["factor"] == QUARTER, 0.25, jnp.where(f["factor"] == WHOLE, 1.0, 4.0))
         for r in range(BLOCKS):
             at = slice(r * rows_of, (r + 1) * rows_of)
-            t = jnp.tanh(
-                (pltpu.matmul_pop(middles[0][r]) + pltpu.matmul_pop(middles[1][r])) + side_sum[at]
-            )
-            new = base[at] + factor * t
+            middle = pltpu.matmul_pop(middles[0][r]) + pltpu.matmul_pop(middles[1][r])
+            side = jnp.concatenate([
+                part[0, h, 7 + r * rows_of:7 + (r + 1) * rows_of, :]
+                + part[1, h, 9 + r * rows_of:9 + (r + 1) * rows_of, :] for h in (0, 1)
+            ], 1)
+            new = base[at] + factor * jnp.tanh(middle + side)
             st[f["dst"], at] = new
             rounded[f["rdst"], WIDTH + r * rows_of:WIDTH + (r + 1) * rows_of, :] = new.astype(bf16)
 

time: 25.1 us -> 24.4 us (0.972)
  Pallas kernels: 23.9 us -> 23.2 us
    pallas_call x1, Pallas kernels: 23.9 us -> 23.2 us  [per_device(): pl.pallas_call(functools.partial(kernel, devices), name='cycle', out_shap...]
where the time goes in v7:
time: 24.4 us; the launch traced here: 24.2 us
  Pallas kernels  23.2 us (95%)
  local copies, waits for them, and re-layouts  0.97 us (4%)
    pallas_call x1, Pallas kernels, per_device(): pl.pallas_call(functools.partial(kernel, devices), name='cycle', out_shap...  23.2 us
    unnamed x1, local copies, waits for them, and re-layouts  0.97 us

profile of v7, /device:TPU:29, one launch (start us, length us, event | category | flops | bytes accessed | tf_op | source)
XLA Modules:
  0.0 24.2 jit_solution(15238207227257259028)
XLA Ops:
  0.0 23.2 %cycle.1 = f32[4,256,256]{2,1,0:T(8,128)S(1)} custom-call(f32[256,256]{1,0:T(8,128)} %x_hbm.1, f32[1,256,256]{2,1,0:T(8,128)} %g_hbm.1, bf16[4,256,2304]{2,1,0:T(8,128)(2,1)} %w_hbm.1), custom_call_target="tpu_custom_call" | custom-call | tf_op jit(solution)/shard_map/cycle/pallas_call | solution.py:527
  23.2 1.0 %copy.5 = f32[4,256,256]{2,1,0:T(8,128)} copy(f32[4,256,256]{2,1,0:T(8,128)S(1)} %cycle.1) | data formatting | bytes 2097152

commit v8 on v7

--- a/solution.py
+++ b/solution.py
@@ -19,7 +19,7 @@
 TO_LEFT, TO_FIRST, TO_SECOND, TO_FINAL, TO_CHANGE, TO_RHS, CHANGE, RHS = range(10, 18)
 ROUNDED = 18
 WEIGHT = ROUNDED
-NOTHING, PSI_OF_LEFT, FIRST_POINT, CHANGES, KEEP, START, PUT_0, OWNER_0, PUT_1, PUT_2, PUT_LAST, OWNER = range(12)
+NOTHING, PSI_OF_LEFT, FIRST_POINT, CHANGES, KEEP, START, PUT_0, OWNER_0, PUT_1, PUT_2, OWNER = range(11)
 FIELDS = ("src", "dst", "w", "add", "factor", "rsrc", "rdst", "by", "recv", "relay", "need", "op")
 BY_ONE, BY_TWO = 0, 1
 QUARTER, WHOLE, FOUR = 0, 1, 2
@@ -50,8 +50,7 @@
     def own(src, dst, **kw):
         return step(src, dst, 0, add=RH, factor=WHOLE, **kw)
 
-    last = [step(OUT, OUT, 1, op=PUT_1), step(OUT, OUT, 2, op=PUT_LAST)]
-    early = [step(OUT, OUT, 1, op=PUT_1), step(OUT, OUT, 2, op=PUT_2)]
+    last = [step(OUT, OUT, 1, op=PUT_1), step(OUT, OUT, 2, op=PUT_2)]
     body = fine(TO_LEFT) + again()
     mate = fine(TO_LEFT) + again(TO_RHS)
     final = [whole(FINAL, LF, relay=1)]
@@ -77,7 +76,7 @@
             own(TMP, TMP, send=TO_SECOND, by=BY_TWO)] + last,
         "mate": mate + [own(LF, CC, recv=FINAL, op=PUT_0)] + last,
         "owner": body + relaxed + owner_second + last,
-        "owner_last": body + relaxed + early + owner_second,
+        "owner_last": body + relaxed + last + owner_second,
     }
 
 
@@ -233,9 +232,6 @@
     part[:, :, 8 + cells:, :] = jnp.zeros((2, 2, 8, half), f32)
     st[ZERO] = jnp.zeros((cells, chans), f32)
 
-    def put(slot, n):
-        o_ref[n] = st[slot].T
-
     def by_rows(body):
         def rows(r, _):
             first = pl.multiple_of(r * ROWS, ROWS)
@@ -272,6 +268,7 @@
         rounded[TO_FINAL, inner_at] = solved.astype(bf16)
         rounded[TO_SECOND, inner_at] = cc.astype(bf16)
         st[CC, at] = solved
+        o_ref[COARSEN - 1, at] = solved
 
     rows_of = cells // BLOCKS
     col = lax.rem(lax.broadcasted_iota(jnp.int32, (rows_of, chans), 0), WIDTH)
@@ -445,6 +442,8 @@
                     t = jnp.where(op == PUT_0, st[f["dst"], at] - base[at], st[TT, at])
                     out = st[LF, at] + 0.25 * t
                     st[OUT, at] = out
+                    o_ref[0, at] = out
+                    o_ref[COARSEN - 1, at] = st[CC, at]
                     rounded[OUTB, inner_at] = out.astype(bf16)
 
                 by_rows(rows)
@@ -460,20 +459,9 @@
                 by_rows(rows)
                 send_solved()
 
-            @pl.when(op >= START)
-            def _():
-                whole_put = op == OWNER
-
-                def one(n, _):
-                    put_last = jnp.logical_or(whole_put, n == 1)
-                    place = jnp.where(op >= PUT_1, op - PUT_1 + 1, 0)
-                    put(
-                        jnp.where(put_last, CC, OUT),
-                        jnp.where(put_last, COARSEN - 1, jnp.minimum(place, COARSEN - 2)),
-                    )
-                    return 0
-
-                lax.fori_loop(0, jnp.where(op == PUT_LAST, 2, 1), one, 0)
+            @pl.when(jnp.logical_or(op == PUT_1, op == PUT_2))
+            def _():
+                o_ref[op - PUT_1 + 1] = st[OUT]
 
             @pl.when(op == CHANGES)
             def _():
@@ -524,10 +512,10 @@
 
 def per_device(devices, inputs, guess, weights):
     chans, cells = inputs.shape
-    return pl.pallas_call(
+    states = pl.pallas_call(
         functools.partial(kernel, devices),
         name="cycle",
-        out_shape=pltpu.VMEM((COARSEN, chans, cells), jnp.float32),
+        out_shape=pltpu.VMEM((COARSEN, cells, chans), jnp.float32),
         in_specs=[pl.BlockSpec(memory_space=pltpu.HBM)] * 3,
         out_specs=pl.BlockSpec(memory_space=pltpu.VMEM),
         scratch_shapes=[
@@ -549,6 +537,7 @@
             collective_id=0, has_side_effects=True, vmem_limit_bytes=56 * 2**20,
         ),
     )(*[pltpu.with_memory_space_constraint(a, pltpu.HBM) for a in (inputs, guess, weights)])
+    return jnp.swapaxes(states, 1, 2)
 
 
 def solution(mesh):

time: 24.4 us -> 24.3 us (level)
  local copies, waits for them, and re-layouts: 0.97 us -> 1.31 us
  Pallas kernels: 23.2 us -> 22.9 us
    transpose x0 -> x1, local copies, waits for them, and re-layouts: none -> 1.31 us  [per_device(): return jnp.swapaxes(states, 1, 2)]
    unnamed x1 -> x0, local copies, waits for them, and re-layouts: 0.97 us -> none
    pallas_call x1, Pallas kernels: 23.2 us -> 22.9 us  [per_device(): pl.pallas_call(functools.partial(kernel, devices), name='cycle', out_shap...]
where the time goes in v8:
time: 24.3 us; the launch traced here: 24.2 us
  Pallas kernels  22.9 us (94%)
  local copies, waits for them, and re-layouts  1.31 us (5%)
    pallas_call x1, Pallas kernels, per_device(): pl.pallas_call(functools.partial(kernel, devices), name='cycle', out_shap...  22.9 us
    transpose x1, local copies, waits for them, and re-layouts, per_device(): return jnp.swapaxes(states, 1, 2)  1.31 us

profile of v8, /device:TPU:29, one launch (start us, length us, event | category | flops | bytes accessed | tf_op | source)
XLA Modules:
  0.0 24.2 jit_solution(9266600718857934281)
XLA Ops:
  0.0 22.9 %cycle.1 = f32[4,256,256]{2,1,0:T(8,128)S(1)} custom-call(f32[256,256]{1,0:T(8,128)} %x_hbm.1, f32[1,256,256]{2,1,0:T(8,128)} %g_hbm.1, bf16[4,256,2304]{2,1,0:T(8,128)(2,1)} %w_hbm.1), custom_call_target="tpu_custom_call" | custom-call | tf_op jit(solution)/shard_map/cycle/pallas_call | solution.py:515
  22.9 1.3 %copy.4 = f32[4,256,256]{2,1,0:T(8,128)} copy(f32[4,256,256]{1,2,0:T(8,128)S(1)} %bitcast.1) | data formatting | bytes 2097152 | tf_op jit(solution)/shard_map/transpose | solution.py:540

commit v9 on v6

--- a/solution.py
+++ b/solution.py
@@ -64,9 +64,9 @@
             step(TMP, XZ, 0, factor=FOUR), whole(FIRST, LF, relay=1, need=1),
             own(LF, CC, op=OWNER_0)] + last,
         "head": fine(TO_LEFT) + again(TO_RHS, FIRST_POINT) + [
-            own(LF, CC, recv=FINAL, op=PUT_0)] + last + [
+            own(LF, CC, recv=FINAL, op=PUT_0),
             step(LF, XZ, COARSEN, factor=FOUR, need=2, rsrc=FINAL),
-            step(TMP, TMP, COARSEN, factor=FOUR, recv=SECOND, op=CHANGES)],
+            step(TMP, TMP, COARSEN, factor=FOUR, recv=SECOND, op=CHANGES)] + last,
         "lead": body + [
             own(LF, TMP, recv=FIRST, send=TO_FIRST, by=BY_TWO),
             whole(FINAL, LF, relay=1, need=1),
@@ -213,7 +213,7 @@
         remote(inner(slot), inner(slot), extra_sem.at[0], recv_sem.at[slot], back).wait_recv()
 
     def weight_to(by):
-        return remote(w.at[0], w.at[COARSEN], extra_sem.at[0], recv_sem.at[WEIGHT], by)
+        return remote(w_hbm.at[0], w.at[COARSEN], extra_sem.at[0], recv_sem.at[WEIGHT], by)
 
     def special(slot, to, by):
         return remote(inner(slot), inner(to), send_sem.at[slot - TO_LEFT], recv_sem.at[to], by)
@@ -263,6 +263,16 @@
 
         st[CC] = solved
 
+    pl.semaphore_wait(barrier, greeted)
+
+    @pl.when(shares)
+    def _():
+        weight_to(1).start()
+
+    @pl.when(owner_shares)
+    def _():
+        weight_to(1 - COARSEN).start()
+
     rows_of = cells // BLOCKS
     col = lax.rem(lax.broadcasted_iota(jnp.int32, (rows_of, chans), 0), WIDTH)
     order = [
@@ -286,18 +296,6 @@
 
     def run(sides, middles, i, fields):
         f = dict(zip(FIELDS, fields))
-
-        @pl.when(i == 1)
-        def _():
-            pl.semaphore_wait(barrier, greeted)
-
-            @pl.when(shares)
-            def _():
-                weight_to(1).start()
-
-            @pl.when(owner_shares)
-            def _():
-                weight_to(1 - COARSEN).start()
 
         received = f["recv"] != NONE
 

time: 24.2 us -> 24 us (level)
  no operation moved by 1% of the time
where the time goes in v9:
time: 24 us; the launch traced here: 23.8 us
  Pallas kernels  22.8 us (95%)
  local copies, waits for them, and re-layouts  0.97 us (4%)
    pallas_call x1, Pallas kernels, per_device(): pl.pallas_call(functools.partial(kernel, devices), name='cycle', out_shap...  22.8 us
    unnamed x1, local copies, waits for them, and re-layouts  0.97 us

profile of v9, /device:TPU:29, one launch (start us, length us, event | category | flops | bytes accessed | tf_op | source)
XLA Modules:
  0.0 23.8 jit_solution(9630981634751196412)
XLA Ops:
  0.0 22.8 %cycle.1 = f32[4,256,256]{2,1,0:T(8,128)S(1)} custom-call(f32[256,256]{1,0:T(8,128)} %x_hbm.1, f32[1,256,256]{2,1,0:T(8,128)} %g_hbm.1, bf16[4,256,2304]{2,1,0:T(8,128)(2,1)} %w_hbm.1), custom_call_target="tpu_custom_call" | custom-call | tf_op jit(solution)/shard_map/cycle/pallas_call | solution.py:481
  22.8 1.0 %copy.5 = f32[4,256,256]{2,1,0:T(8,128)} copy(f32[4,256,256]{2,1,0:T(8,128)S(1)} %cycle.1) | data formatting | bytes 2097152

commit v10 on v7

--- a/solution.py
+++ b/solution.py
@@ -66,9 +66,9 @@
             step(TMP, XZ, 0, factor=FOUR), whole(FIRST, LF, relay=1, need=1),
             own(LF, CC, op=OWNER_0)] + last,
         "head": fine(TO_LEFT) + again(TO_RHS, FIRST_POINT) + [
-            own(LF, CC, recv=FINAL, op=PUT_0)] + last + [
+            own(LF, CC, recv=FINAL, op=PUT_0),
             step(LF, XZ, COARSEN, factor=FOUR, need=2, rsrc=FINAL),
-            step(TMP, TMP, COARSEN, factor=FOUR, recv=SECOND, op=CHANGES)],
+            step(TMP, TMP, COARSEN, factor=FOUR, recv=SECOND, op=CHANGES)] + last,
         "lead": body + [
             own(LF, TMP, recv=FIRST, send=TO_FIRST, by=BY_TWO),
             whole(FINAL, LF, relay=1, need=1),
@@ -215,7 +215,7 @@
         remote(inner(slot), inner(slot), extra_sem.at[0], recv_sem.at[slot], back).wait_recv()
 
     def weight_to(by):
-        return remote(w.at[0], w.at[COARSEN], extra_sem.at[0], recv_sem.at[WEIGHT], by)
+        return remote(w_hbm.at[0], w.at[COARSEN], extra_sem.at[0], recv_sem.at[WEIGHT], by)
 
     def special(slot, to, by):
         return remote(inner(slot), inner(to), send_sem.at[slot - TO_LEFT], recv_sem.at[to], by)
@@ -273,6 +273,12 @@
         rounded[TO_SECOND, inner_at] = cc.astype(bf16)
         st[CC, at] = solved
 
+    pl.semaphore_wait(barrier, greeted)
+
+    @pl.when(owner_shares)
+    def _():
+        weight_to(1 - COARSEN).start()
+
     rows_of = cells // BLOCKS
     col = lax.rem(lax.broadcasted_iota(jnp.int32, (rows_of, chans), 0), WIDTH)
     order = [
@@ -297,17 +303,9 @@
     def run(sides, middles, i, fields):
         f = dict(zip(FIELDS, fields))
 
-        @pl.when(i == 1)
-        def _():
-            pl.semaphore_wait(barrier, greeted)
-
-            @pl.when(shares)
-            def _():
-                weight_to(1).start()
-
-            @pl.when(owner_shares)
-            def _():
-                weight_to(1 - COARSEN).start()
+        @pl.when(jnp.logical_and(i == 1, shares))
+        def _():
+            weight_to(1).start()
 
         received = f["recv"] != NONE
 

time: 24.4 us -> 24 us (0.984)
  Pallas kernels: 23.2 us -> 22.8 us
    pallas_call x1, Pallas kernels: 23.2 us -> 22.8 us  [per_device(): pl.pallas_call(functools.partial(kernel, devices), name='cycle', out_shap...]
where the time goes in v10:
time: 24 us; the launch traced here: 23.8 us
  Pallas kernels  22.8 us (95%)
  local copies, waits for them, and re-layouts  0.97 us (4%)
    pallas_call x1, Pallas kernels, per_device(): pl.pallas_call(functools.partial(kernel, devices), name='cycle', out_shap...  22.8 us
    unnamed x1, local copies, waits for them, and re-layouts  0.97 us

profile of v10, /device:TPU:29, one launch (start us, length us, event | category | flops | bytes accessed | tf_op | source)
XLA Modules:
  0.0 23.8 jit_solution(7194514208308022491)
XLA Ops:
  0.0 22.8 %cycle.1 = f32[4,256,256]{2,1,0:T(8,128)S(1)} custom-call(f32[256,256]{1,0:T(8,128)} %x_hbm.1, f32[1,256,256]{2,1,0:T(8,128)} %g_hbm.1, bf16[4,256,2304]{2,1,0:T(8,128)(2,1)} %w_hbm.1), custom_call_target="tpu_custom_call" | custom-call | tf_op jit(solution)/shard_map/cycle/pallas_call | solution.py:525
  22.8 1.0 %copy.5 = f32[4,256,256]{2,1,0:T(8,128)} copy(f32[4,256,256]{2,1,0:T(8,128)S(1)} %cycle.1) | data formatting | bytes 2097152

commit v11 on v9

--- a/solution.py
+++ b/solution.py
@@ -18,7 +18,7 @@
 TO_LEFT, TO_FIRST, TO_SECOND, TO_FINAL, TO_CHANGE, TO_RHS, CHANGE, RHS = range(10, 18)
 ROUNDED = 18
 WEIGHT = ROUNDED
-NOTHING, PSI_OF_LEFT, FIRST_POINT, START, PUT_0, PUT_1, PUT_2, OWNER_0, OWNER, CHANGES, KEEP = range(11)
+NOTHING, PSI_OF_LEFT, FIRST_POINT, START, PUT_0, PUT_1, PUT_2, PUT_OUT, OWNER_0, OWNER, CHANGES, KEEP = range(12)
 FIELDS = ("src", "dst", "w", "add", "factor", "rsrc", "rdst", "by", "recv", "relay", "need", "op")
 BY_ONE, BY_TWO = 0, 1
 QUARTER, WHOLE, FOUR = 0, 1, 2
@@ -55,14 +55,14 @@
     final = [whole(FINAL, LF, relay=1)]
     owner_second = [whole(SECOND, TMP), step(TMP, PSI, 0, factor=WHOLE, op=OWNER)]
     relaxed = [whole(FIRST, TMP, need=1), own(TMP, CC)] + final + [
-        step(LF, DUMP, 0, factor=WHOLE, op=PUT_0)]
+        step(LF, OUT, 0, op=PUT_OUT)]
     return {
         "start": fine(TO_LEFT, KEEP, START) + last,
         "lead_first": body + [own(LF, CC, recv=FIRST, send=TO_FIRST, by=BY_TWO, op=PUT_0)] + last,
         "mate_first": mate + [own(LF, CC, recv=FIRST, op=PUT_0)] + last,
         "owner_first": body + [
             step(TMP, XZ, 0, factor=FOUR), whole(FIRST, LF, relay=1, need=1),
-            own(LF, CC, op=OWNER_0)] + last,
+            own(LF, CC, send=TO_SECOND, op=OWNER_0)] + last,
         "head": fine(TO_LEFT) + again(TO_RHS, FIRST_POINT) + [
             own(LF, CC, recv=FINAL, op=PUT_0),
             step(LF, XZ, COARSEN, factor=FOUR, need=2, rsrc=FINAL),
@@ -249,19 +249,11 @@
         st[TMP] = start
         rounded_store(TMPB, start)
 
-    def finish_owner(xy):
-        cc = st[CC]
-        second = st[RH] - (cc - st[PSI])
-        solved = st[XZ] + ((cc - st[xy]) + second)
-
+    def send_solved():
         @pl.when(lead_next)
         def _():
-            rounded_store(TO_FINAL, solved)
             special(TO_FINAL, FINAL, 2).start()
-            rounded_store(TO_SECOND, cc)
             special(TO_SECOND, SECOND, 2).start()
-
-        st[CC] = solved
 
     pl.semaphore_wait(barrier, greeted)
 
@@ -373,7 +365,9 @@
             st[f["dst"], at] = new
             rounded[f["rdst"], WIDTH + r * rows_of:WIDTH + (r + 1) * rows_of, :] = new.astype(bf16)
 
-        @pl.when(jnp.logical_and(f["rdst"] > UNSENT, has_next))
+        @pl.when(jnp.logical_and(
+            jnp.logical_and(f["rdst"] > UNSENT, has_next), f["op"] != OWNER_0
+        ))
         def _():
             message(f["rdst"], distance(f["by"])).start()
 
@@ -407,10 +401,18 @@
 
             @pl.when(op == OWNER_0)
             def _():
-                t = st[CC] - base[...]
-                st[TT] = t
-                st[PSI] = st[LF] + t
-                finish_owner(XZ)
+                for r in range(4):
+                    at = slice(r * cells // 4, (r + 1) * cells // 4)
+                    cc, xi = st[CC, at], st[XZ, at]
+                    psi = st[LF, at] + (cc - base[at])
+                    solved = xi + ((cc - xi) + (st[RH, at] - (cc - psi)))
+                    rounded[TO_FINAL, WIDTH + at.start:WIDTH + at.stop, :] = solved.astype(bf16)
+                    st[PSI, at] = solved
+                send_solved()
+                for r in range(4):
+                    at = slice(r * cells // 4, (r + 1) * cells // 4)
+                    st[TT, at] = st[CC, at] - base[at]
+                    st[CC, at] = st[PSI, at]
 
             @pl.when(jnp.logical_or(op == PUT_0, jnp.logical_or(op == START, op == OWNER_0)))
             def _():
@@ -428,8 +430,17 @@
             @pl.when(op == OWNER)
             def _():
                 arrived(CHANGE)
-                st[XZ] = rounded[CHANGE, WIDTH:WIDTH + cells, :].astype(f32)
-                finish_owner(ZERO)
+                for r in range(4):
+                    at = slice(r * cells // 4, (r + 1) * cells // 4)
+                    inner_at = slice(WIDTH + at.start, WIDTH + at.stop)
+                    cc = st[CC, at]
+                    change = rounded[CHANGE, inner_at, :].astype(f32)
+                    second = st[RH, at] - (cc - st[PSI, at])
+                    solved = change + ((cc - st[ZERO, at]) + second)
+                    rounded[TO_SECOND, inner_at, :] = cc.astype(bf16)
+                    rounded[TO_FINAL, inner_at, :] = solved.astype(bf16)
+                    st[CC, at] = solved
+                send_solved()
 
             @pl.when(op == CHANGES)
             def _():

time: 24 us -> 23.6 us (0.983)
  Pallas kernels: 22.8 us -> 22.4 us
    pallas_call x1, Pallas kernels: 22.8 us -> 22.4 us  [per_device(): pl.pallas_call(functools.partial(kernel, devices), name='cycle', out_shap...]
where the time goes in v11:
time: 23.6 us; the launch traced here: 23.4 us
  Pallas kernels  22.4 us (95%)
  local copies, waits for them, and re-layouts  0.97 us (4%)
    pallas_call x1, Pallas kernels, per_device(): pl.pallas_call(functools.partial(kernel, devices), name='cycle', out_shap...  22.4 us
    unnamed x1, local copies, waits for them, and re-layouts  0.97 us

profile of v11, /device:TPU:29, one launch (start us, length us, event | category | flops | bytes accessed | tf_op | source)
XLA Modules:
  0.0 23.4 jit_solution(5707284603943967608)
XLA Ops:
  0.0 22.4 %cycle.1 = f32[4,256,256]{2,1,0:T(8,128)S(1)} custom-call(f32[256,256]{1,0:T(8,128)} %x_hbm.1, f32[1,256,256]{2,1,0:T(8,128)} %g_hbm.1, bf16[4,256,2304]{2,1,0:T(8,128)(2,1)} %w_hbm.1), custom_call_target="tpu_custom_call" | custom-call | tf_op jit(solution)/shard_map/cycle/pallas_call | solution.py:492
  22.4 1.0 %copy.5 = f32[4,256,256]{2,1,0:T(8,128)} copy(f32[4,256,256]{2,1,0:T(8,128)S(1)} %cycle.1) | data formatting | bytes 2097152

commit v12 on v11

--- a/solution.py
+++ b/solution.py
@@ -231,8 +231,8 @@
     part[:, :, 8 + cells:, :] = jnp.zeros((2, 2, 8, half), f32)
     st[ZERO] = jnp.zeros((cells, chans), f32)
 
-    def put(n):
-        o_ref[n] = st[OUT].T
+    def put(slot, n):
+        o_ref[n] = st[slot].T
 
     own_load.wait()
     for load in weight_loads(2):
@@ -421,12 +421,6 @@
                 st[OUT] = out
                 rounded_store(OUTB, out)
 
-            put_at = jnp.where(op == PUT_1, 1, jnp.where(op == PUT_2, 2, 0))
-
-            @pl.when(jnp.logical_and(op >= START, op <= OWNER_0))
-            def _():
-                put(put_at)
-
             @pl.when(op == OWNER)
             def _():
                 arrived(CHANGE)
@@ -442,6 +436,14 @@
                     st[CC, at] = solved
                 send_solved()
 
+            put_at = jnp.where(
+                op == OWNER, COARSEN - 1, jnp.where(op == PUT_1, 1, jnp.where(op == PUT_2, 2, 0))
+            )
+
+            @pl.when(jnp.logical_and(op >= START, op <= OWNER))
+            def _():
+                put(jnp.where(op == OWNER, CC, OUT), put_at)
+
             @pl.when(op == CHANGES)
             def _():
                 rounded_store(TO_CHANGE, st[XZ] - st[TMP])
@@ -460,31 +462,37 @@
         lax.fori_loop(0, count, functools.partial(run, sides, middles), fields_of(0))
         for m in (0, 1):
             pltpu.matmul_acc_lhs(sides[m][0], rounded[CPB, 0:rows_of, :], 0)
+        finish()
+        for m in (0, 1):
             side_sum[0:rows_of, :] = pltpu.matmul_pop(sides[m][0])
+
+    def finish():
+        @pl.when(jnp.logical_not(jnp.logical_and(owner_shares, last_owner)))
+        def _():
+            put(CC, COARSEN - 1)
+
+        def drain(copy, cond):
+            @pl.when(cond)
+            def _():
+                copy.wait_send()
+
+        relaxed = jnp.logical_or(
+            jnp.logical_and(owner, lead_next), jnp.logical_and(phase == 1, group > 0)
+        )
+        drain(weight_to(back), jnp.logical_or(shares, owner_shares))
+        drain(special(TO_LEFT, LEFT, back), has_next)
+        drain(special(TO_RHS, RHS, back), shares)
+        drain(special(TO_FIRST, FIRST, back), phase < 2)
+        drain(special(TO_FINAL, FINAL, back), relaxed)
+        drain(special(TO_SECOND, SECOND, back), relaxed)
+        drain(special(TO_CHANGE, CHANGE, back), changes)
+        drain(relay_of(FIRST), first_owner)
+        drain(relay_of(FINAL), jnp.logical_and(lead, group > 0))
+        drain(relay_of(SECOND), jnp.logical_and(phase == 1, group > 0))
 
     pl.run_scoped(
         loop, *[pltpu.ACC(m)((rows_of, chans), f32) for m in (0, 1) for _ in range(2 * BLOCKS)]
     )
-    o_ref[COARSEN - 1] = st[CC].T
-
-    def drain(copy, cond):
-        @pl.when(cond)
-        def _():
-            copy.wait_send()
-
-    relaxed = jnp.logical_or(
-        jnp.logical_and(owner, lead_next), jnp.logical_and(phase == 1, group > 0)
-    )
-    drain(weight_to(back), jnp.logical_or(shares, owner_shares))
-    drain(special(TO_LEFT, LEFT, back), has_next)
-    drain(special(TO_RHS, RHS, back), shares)
-    drain(special(TO_FIRST, FIRST, back), phase < 2)
-    drain(special(TO_FINAL, FINAL, back), relaxed)
-    drain(special(TO_SECOND, SECOND, back), relaxed)
-    drain(special(TO_CHANGE, CHANGE, back), changes)
-    drain(relay_of(FIRST), first_owner)
-    drain(relay_of(FINAL), jnp.logical_and(lead, group > 0))
-    drain(relay_of(SECOND), jnp.logical_and(phase == 1, group > 0))
 
 
 def per_device(devices, inputs, guess, weights):

time: 23.6 us -> 23.7 us (level)
  no operation moved by 1% of the time
where the time goes in v12:
time: 23.7 us; the launch traced here: 23.5 us
  Pallas kernels  22.5 us (95%)
  local copies, waits for them, and re-layouts  0.97 us (4%)
    pallas_call x1, Pallas kernels, per_device(): pl.pallas_call(functools.partial(kernel, devices), name='cycle', out_shap...  22.5 us
    unnamed x1, local copies, waits for them, and re-layouts  0.97 us

profile of v12, /device:TPU:29, one launch (start us, length us, event | category | flops | bytes accessed | tf_op | source)
XLA Modules:
  0.0 23.5 jit_solution(18189708422791946985)
XLA Ops:
  0.0 22.5 %cycle.1 = f32[4,256,256]{2,1,0:T(8,128)S(1)} custom-call(f32[256,256]{1,0:T(8,128)} %x_hbm.1, f32[1,256,256]{2,1,0:T(8,128)} %g_hbm.1, bf16[4,256,2304]{2,1,0:T(8,128)(2,1)} %w_hbm.1), custom_call_target="tpu_custom_call" | custom-call | tf_op jit(solution)/shard_map/cycle/pallas_call | solution.py:500
  22.5 1.0 %copy.5 = f32[4,256,256]{2,1,0:T(8,128)} copy(f32[4,256,256]{2,1,0:T(8,128)S(1)} %cycle.1) | data formatting | bytes 2097152

commit v13 on v12

--- a/solution.py
+++ b/solution.py
@@ -64,9 +64,10 @@
             step(TMP, XZ, 0, factor=FOUR), whole(FIRST, LF, relay=1, need=1),
             own(LF, CC, send=TO_SECOND, op=OWNER_0)] + last,
         "head": fine(TO_LEFT) + again(TO_RHS, FIRST_POINT) + [
-            own(LF, CC, recv=FINAL, op=PUT_0),
+            own(LF, CC, recv=FINAL),
             step(LF, XZ, COARSEN, factor=FOUR, need=2, rsrc=FINAL),
-            step(TMP, TMP, COARSEN, factor=FOUR, recv=SECOND, op=CHANGES)] + last,
+            step(TMP, TMP, COARSEN, factor=FOUR, recv=SECOND, op=CHANGES),
+            step(LF, OUT, 0, rsrc=FINAL, op=PUT_OUT)] + last,
         "lead": body + [
             own(LF, TMP, recv=FIRST, send=TO_FIRST, by=BY_TWO),
             whole(FINAL, LF, relay=1, need=1),
@@ -234,6 +235,12 @@
     def put(slot, n):
         o_ref[n] = st[slot].T
 
+    pl.semaphore_wait(barrier, greeted)
+
+    @pl.when(owner_shares)
+    def _():
+        weight_to(1 - COARSEN).start()
+
     own_load.wait()
     for load in weight_loads(2):
         load.start()
@@ -255,15 +262,9 @@
             special(TO_FINAL, FINAL, 2).start()
             special(TO_SECOND, SECOND, 2).start()
 
-    pl.semaphore_wait(barrier, greeted)
-
     @pl.when(shares)
     def _():
         weight_to(1).start()
-
-    @pl.when(owner_shares)
-    def _():
-        weight_to(1 - COARSEN).start()
 
     rows_of = cells // BLOCKS
     col = lax.rem(lax.broadcasted_iota(jnp.int32, (rows_of, chans), 0), WIDTH)

time: 23.7 us -> 23.6 us (level)
  no operation moved by 1% of the time
where the time goes in v13:
time: 23.6 us; the launch traced here: 23.5 us
  Pallas kernels  22.5 us (95%)
  local copies, waits for them, and re-layouts  0.97 us (4%)
    pallas_call x1, Pallas kernels, per_device(): pl.pallas_call(functools.partial(kernel, devices), name='cycle', out_shap...  22.5 us
    unnamed x1, local copies, waits for them, and re-layouts  0.97 us

profile of v13, /device:TPU:29, one launch (start us, length us, event | category | flops | bytes accessed | tf_op | source)
XLA Modules:
  0.0 23.5 jit_solution(17453310614977463891)
XLA Ops:
  0.0 22.5 %cycle.1 = f32[4,256,256]{2,1,0:T(8,128)S(1)} custom-call(f32[256,256]{1,0:T(8,128)} %x_hbm.1, f32[1,256,256]{2,1,0:T(8,128)} %g_hbm.1, bf16[4,256,2304]{2,1,0:T(8,128)(2,1)} %w_hbm.1), custom_call_target="tpu_custom_call" | custom-call | tf_op jit(solution)/shard_map/cycle/pallas_call | solution.py:501
  22.5 1.0 %copy.5 = f32[4,256,256]{2,1,0:T(8,128)} copy(f32[4,256,256]{2,1,0:T(8,128)S(1)} %cycle.1) | data formatting | bytes 2097152

commit v14 on v13

--- a/solution.py
+++ b/solution.py
@@ -290,6 +290,11 @@
     def run(sides, middles, i, fields):
         f = dict(zip(FIELDS, fields))
 
+        @pl.when(f["need"] == 1)
+        def _():
+            arrived(RHS)
+            st[RHM] = rounded[RHS, WIDTH:WIDTH + cells, :].astype(f32)
+
         received = f["recv"] != NONE
 
         @pl.when(received)
@@ -324,7 +329,7 @@
         def _():
             st[f["src"]] = rounded[source, WIDTH:WIDTH + cells, :].astype(f32)
 
-        @pl.when(jnp.logical_or(i < COARSEN - 1, jnp.logical_or(next_weight, f["need"] > 0)))
+        @pl.when(jnp.logical_or(i < COARSEN - 1, next_weight))
         def _():
             @pl.when(i < COARSEN - 1)
             def _():
@@ -333,11 +338,6 @@
             @pl.when(next_weight)
             def _():
                 remote(w.at[0], w.at[COARSEN], extra_sem.at[0], recv_sem.at[WEIGHT], back).wait_recv()
-
-            @pl.when(f["need"] == 1)
-            def _():
-                arrived(RHS)
-                st[RHM] = rounded[RHS, WIDTH:WIDTH + cells, :].astype(f32)
 
         for k in range(1, 5):
             for m in (0, 1):
@@ -379,7 +379,6 @@
             @pl.when(op == PSI_OF_LEFT)
             def _():
                 psi = st[LF] + 4.0 * (st[CC] - base[...])
-                st[PSI] = psi
                 st[QQ] = (st[CP] - psi) - st[CP]
 
             @pl.when(op == KEEP)
@@ -397,7 +396,7 @@
 
             @pl.when(op == FIRST_POINT)
             def _():
-                rounded_store(TO_FIRST, st[PSI] + st[RH])
+                rounded_store(TO_FIRST, (st[CP] - (st[QQ] + st[CP])) + st[RH])
                 special(TO_FIRST, FIRST, 1).start()
 
             @pl.when(op == OWNER_0)

time: 23.6 us -> 23.6 us (level)
  no operation moved by 1% of the time
where the time goes in v14:
time: 23.6 us; the launch traced here: 23.5 us
  Pallas kernels  22.5 us (95%)
  local copies, waits for them, and re-layouts  0.97 us (4%)
    pallas_call x1, Pallas kernels, per_device(): pl.pallas_call(functools.partial(kernel, devices), name='cycle', out_shap...  22.5 us
    unnamed x1, local copies, waits for them, and re-layouts  0.97 us

profile of v14, /device:TPU:29, one launch (start us, length us, event | category | flops | bytes accessed | tf_op | source)
XLA Modules:
  0.0 23.5 jit_solution(927445891324640708)
XLA Ops:
  0.0 22.5 %cycle.1 = f32[4,256,256]{2,1,0:T(8,128)S(1)} custom-call(f32[256,256]{1,0:T(8,128)} %x_hbm.1, f32[1,256,256]{2,1,0:T(8,128)} %g_hbm.1, bf16[4,256,2304]{2,1,0:T(8,128)(2,1)} %w_hbm.1), custom_call_target="tpu_custom_call" | custom-call | tf_op jit(solution)/shard_map/cycle/pallas_call | solution.py:500
  22.5 1.0 %copy.5 = f32[4,256,256]{2,1,0:T(8,128)} copy(f32[4,256,256]{2,1,0:T(8,128)S(1)} %cycle.1) | data formatting | bytes 2097152

commit v15 on v14

--- a/solution.py
+++ b/solution.py
@@ -235,12 +235,6 @@
     def put(slot, n):
         o_ref[n] = st[slot].T
 
-    pl.semaphore_wait(barrier, greeted)
-
-    @pl.when(owner_shares)
-    def _():
-        weight_to(1 - COARSEN).start()
-
     own_load.wait()
     for load in weight_loads(2):
         load.start()
@@ -261,6 +255,12 @@
         def _():
             special(TO_FINAL, FINAL, 2).start()
             special(TO_SECOND, SECOND, 2).start()
+
+    pl.semaphore_wait(barrier, greeted)
+
+    @pl.when(owner_shares)
+    def _():
+        weight_to(1 - COARSEN).start()
 
     @pl.when(shares)
     def _():

time: 23.6 us -> 23.6 us (level)
  no operation moved by 1% of the time
where the time goes in v15:
time: 23.6 us; the launch traced here: 23.5 us
  Pallas kernels  22.5 us (95%)
  local copies, waits for them, and re-layouts  0.97 us (4%)
    pallas_call x1, Pallas kernels, per_device(): pl.pallas_call(functools.partial(kernel, devices), name='cycle', out_shap...  22.5 us
    unnamed x1, local copies, waits for them, and re-layouts  0.97 us

profile of v15, /device:TPU:29, one launch (start us, length us, event | category | flops | bytes accessed | tf_op | source)
XLA Modules:
  0.0 23.5 jit_solution(15517990659279677711)
XLA Ops:
  0.0 22.5 %cycle.1 = f32[4,256,256]{2,1,0:T(8,128)S(1)} custom-call(f32[256,256]{1,0:T(8,128)} %x_hbm.1, f32[1,256,256]{2,1,0:T(8,128)} %g_hbm.1, bf16[4,256,2304]{2,1,0:T(8,128)(2,1)} %w_hbm.1), custom_call_target="tpu_custom_call" | custom-call | tf_op jit(solution)/shard_map/cycle/pallas_call | solution.py:500
  22.5 1.0 %copy.5 = f32[4,256,256]{2,1,0:T(8,128)} copy(f32[4,256,256]{2,1,0:T(8,128)S(1)} %cycle.1) | data formatting | bytes 2097152

commit v16 on v14

--- a/solution.py
+++ b/solution.py
@@ -424,6 +424,11 @@
             @pl.when(op == OWNER)
             def _():
                 arrived(CHANGE)
+
+                @pl.when(lead_next)
+                def _():
+                    rounded_store(TO_SECOND, st[CC])
+
                 for r in range(4):
                     at = slice(r * cells // 4, (r + 1) * cells // 4)
                     inner_at = slice(WIDTH + at.start, WIDTH + at.stop)
@@ -431,9 +436,12 @@
                     change = rounded[CHANGE, inner_at, :].astype(f32)
                     second = st[RH, at] - (cc - st[PSI, at])
                     solved = change + ((cc - st[ZERO, at]) + second)
-                    rounded[TO_SECOND, inner_at, :] = cc.astype(bf16)
-                    rounded[TO_FINAL, inner_at, :] = solved.astype(bf16)
                     st[CC, at] = solved
+
+                @pl.when(lead_next)
+                def _():
+                    rounded_store(TO_FINAL, st[CC])
+
                 send_solved()
 
             put_at = jnp.where(

time: 23.6 us -> 23.6 us (level)
  no operation moved by 1% of the time
where the time goes in v16:
time: 23.6 us; the launch traced here: 23.4 us
  Pallas kernels  22.4 us (95%)
  local copies, waits for them, and re-layouts  0.97 us (4%)
    pallas_call x1, Pallas kernels, per_device(): pl.pallas_call(functools.partial(kernel, devices), name='cycle', out_shap...  22.4 us
    unnamed x1, local copies, waits for them, and re-layouts  0.97 us

profile of v16, /device:TPU:29, one launch (start us, length us, event | category | flops | bytes accessed | tf_op | source)
XLA Modules:
  0.0 23.4 jit_solution(4756454541542636071)
XLA Ops:
  0.0 22.4 %cycle.1 = f32[4,256,256]{2,1,0:T(8,128)S(1)} custom-call(f32[256,256]{1,0:T(8,128)} %x_hbm.1, f32[1,256,256]{2,1,0:T(8,128)} %g_hbm.1, bf16[4,256,2304]{2,1,0:T(8,128)(2,1)} %w_hbm.1), custom_call_target="tpu_custom_call" | custom-call | tf_op jit(solution)/shard_map/cycle/pallas_call | solution.py:508
  22.5 1.0 %copy.5 = f32[4,256,256]{2,1,0:T(8,128)} copy(f32[4,256,256]{2,1,0:T(8,128)S(1)} %cycle.1) | data formatting | bytes 2097152
